TPU v7x, 32 devices: a whole 2x2x4 slice. The times are simulated.
32 devices in a mesh: seq: 8 (over y, x, core), fsdp: 4 (over z).
Axes of the slice: x: 2, y: 2, z: 4, core: 2. Of those that a mesh axis runs over, the one named last changes fastest.
Arguments:
- tokens: bfloat16 [8192, 768], P(('seq', 'fsdp')), may hold values from -6 to 6
- query_small: bfloat16 [768, 512], P(('seq', 'fsdp')), may hold values from -0.21875 to 0.21875
- key_small: bfloat16 [768, 512], P(('seq', 'fsdp')), may hold values from -0.21875 to 0.21875
- value_small: bfloat16 [768, 512], P(('seq', 'fsdp')), may hold values from -0.21875 to 0.21875
- out_small: bfloat16 [512, 768], P(None, ('seq', 'fsdp')), may hold values from -1.5 to 1.5
- query_large: bfloat16 [768, 768], P(('seq', 'fsdp')), may hold values from -0.21875 to 0.21875
- key_large: bfloat16 [768, 768], P(('seq', 'fsdp')), may hold values from -0.21875 to 0.21875
- value_large: bfloat16 [768, 768], P(('seq', 'fsdp')), may hold values from -0.21875 to 0.21875
- out_large: bfloat16 [768, 768], P(None, ('seq', 'fsdp')), may hold values from -1.25 to 1.25
- attend_gain: bfloat16 [768], P(('seq', 'fsdp')), may hold values from 0.5 to 1.5
- attend_router: bfloat16 [768], P(('seq', 'fsdp')), may hold values from -0.15625 to 0.15625
- gate_small: bfloat16 [768, 1024], P(('seq', 'fsdp')), may hold values from -0.21875 to 0.21875
- up_small: bfloat16 [768, 1024], P(('seq', 'fsdp')), may hold values from -0.21875 to 0.21875
- down_small: bfloat16 [1024, 768], P(None, ('seq', 'fsdp')), may hold values from -0.1875 to 0.1875
- gate_large: bfloat16 [768, 4096], P(('seq', 'fsdp')), may hold values from -0.21875 to 0.21875
- up_large: bfloat16 [768, 4096], P(('seq', 'fsdp')), may hold values from -0.21875 to 0.21875
- down_large: bfloat16 [4096, 768], P(None, ('seq', 'fsdp')), may hold values from -0.09375 to 0.09375
- feed_gain: bfloat16 [768], P(('seq', 'fsdp')), may hold values from 0.5 to 1.5
- feed_router: bfloat16 [768], P(('seq', 'fsdp')), may hold values from -0.15625 to 0.15625
- lengths: int32 [2], replicated, may hold values from 256 to 7936, as said below
- query_route: int32 [32, 32], replicated, may hold values from 0 to 256, as said below
- key_route: int32 [32, 32], replicated, may hold values from 0 to 256, as said below
- feed_route: int32 [32, 32], P(('seq', 'fsdp')), may hold values from 0 to 256, as said below
- cotangent: bfloat16 [8192, 768], P(('seq', 'fsdp')), may hold values from -6 to 6
Outputs:
- result: bfloat16 [8192, 768], P(('seq', 'fsdp'))
- tokens_grad: float32 [8192, 768], P(('seq', 'fsdp'))
- query_small_grad: float32 [768, 512], P(('seq', 'fsdp'))
- key_small_grad: float32 [768, 512], P(('seq', 'fsdp'))
- value_small_grad: float32 [768, 512], P(('seq', 'fsdp'))
- out_small_grad: float32 [512, 768], P(None, ('seq', 'fsdp'))
- query_large_grad: float32 [768, 768], P(('seq', 'fsdp'))
- key_large_grad: float32 [768, 768], P(('seq', 'fsdp'))
- value_large_grad: float32 [768, 768], P(('seq', 'fsdp'))
- out_large_grad: float32 [768, 768], P(None, ('seq', 'fsdp'))
- attend_gain_grad: float32 [768], P(('seq', 'fsdp'))
- attend_router_grad: float32 [768], P(('seq', 'fsdp'))
- gate_small_grad: float32 [768, 1024], P(('seq', 'fsdp'))
- up_small_grad: float32 [768, 1024], P(('seq', 'fsdp'))
- down_small_grad: float32 [1024, 768], P(None, ('seq', 'fsdp'))
- gate_large_grad: float32 [768, 4096], P(('seq', 'fsdp'))
- up_large_grad: float32 [768, 4096], P(('seq', 'fsdp'))
- down_large_grad: float32 [4096, 768], P(None, ('seq', 'fsdp'))
- feed_gain_grad: float32 [768], P(('seq', 'fsdp'))
- feed_router_grad: float32 [768], P(('seq', 'fsdp'))
Inputs may be any that keep to these rules, and one draw needn't show every extreme that they name: `lengths`: entry 1 (the short document) lies between 256 and 512; both entries together leave at most 128 padding tokens at the end of the pack. `query_route`: row b lists distinct live positions inside aligned block b of 256 tokens, filled slots first and 256 in empty ones; every block with a live token has at least one; in every draw some block fills all 32. `key_route`: row b lists distinct live positions inside aligned block b of 256 tokens, filled slots first and 256 in empty ones; every block with a live token has at least one; in every draw some block fills all 32. `feed_route`: row b lists distinct live positions inside aligned block b of 256 tokens, filled slots first and 256 in empty ones; every block with a live token has at least one; in every draw some block fills all 32.
All inputs are finite; a program needn't handle non-finite values.
Results may differ from a plain program's by a relative error of at most 0.014.
Values may be sent and summed in bfloat16 or wider, within the bound.
No kernel may reach another device: no remote copies, remote signals or barrier semaphores. Data moves between devices by JAX's collectives and lax.ppermute only.
A program may use at most 256 MiB of HBM per device.

v0:
```python
import functools
import math

import jax
import jax.numpy as jnp
from jax import lax
from jax.experimental import pallas as pl
from jax.experimental.pallas import tpu as pltpu
from jax.sharding import PartitionSpec as P

HL = 8
HDL = 64
HH = 12
HDH = 64
RADIUS = 128

NEG = -1e30
EPS = 1e-06
HIGH = lax.Precision.HIGHEST
AXES = ("seq", "fsdp")
F32 = jnp.float32
BF16 = jnp.bfloat16
ROOM = 12 << 20
LENGTHS = {
    "select": 60,
    "weave": 20,
    "light_forward": 60,
    "heavy_pairs": 60,
    "expert": 60,
    "feed": 60,
    "feed_weight": 20,
    "turn": 5.6,
    "routed": 60,
    "settle_third": 12,
}


def declared(name):
    flops = int(LENGTHS.get(name, 0.05) * 1e9)
    return pl.CostEstimate(flops=flops, bytes_accessed=10**10, transcendentals=0)


class Columns:
    def __init__(self, array, start, stop):
        self.array, self.start, self.stop = array, start, stop


def dot(left, right, dims):
    return lax.dot_general(left, right, (dims, ((), ())), preferred_element_type=F32)


def nn(left, right):
    return dot(left, right, ((1,), (0,)))


def nt(left, right):
    return dot(left, right, ((1,), (1,)))


def tn(left, right):
    return dot(left, right, ((0,), (0,)))


def reverse_bits(value, count):
    out = value * 0
    for j in range(count):
        out = out | (((value >> j) & 1) << (count - 1 - j))
    return out


class Net:
    def __init__(self):
        self.seq = lax.axis_size("seq")
        self.depth = lax.axis_size("fsdp")
        self.levels = (self.seq // 2).bit_length() - 1
        self.count = self.seq * self.depth
        s = lax.axis_index("seq")
        self.core, self.pair = s & 1, s >> 1
        self.z = lax.axis_index("fsdp")
        self.device = s * self.depth + self.z

    def pairs(self, move):
        out = []
        for s in range(self.seq):
            for z in range(self.depth):
                pair, core, to_z = move(s >> 1, s & 1, z)
                out.append((s * self.depth + z, (pair * 2 + core) * self.depth + to_z))
        return out

    def by_core(self, array):
        return lax.ppermute(array, AXES, self.pairs(lambda p, c, z: (p, 1 - c, z)))

    def by_bit(self, array, j):
        top = self.levels - 1 - j
        return lax.ppermute(
            array, AXES, self.pairs(lambda p, c, z: (p ^ (1 << (j if c else top)), c, z))
        )

    def by_z(self, array, k):
        return lax.ppermute(array, AXES, self.pairs(lambda p, c, z: (p, c, z ^ k)))

    def target(self, relative):
        zr = relative % self.depth
        bits = (relative // self.depth) % (self.seq // 2)
        core = self.core ^ (relative // (self.count // 2))
        pair = self.pair ^ jnp.where(core == 1, bits, reverse_bits(bits, self.levels))
        return (pair * 2 + core) * self.depth + (self.z ^ zr)

    def from_z(self, shard):
        return [shard] + [self.by_z(shard, k) for k in range(1, self.depth)]

    def exchange_z(self, pieces):
        return [pieces[0]] + [self.by_z(pieces[k], k) for k in range(1, self.depth)]

    def gather(self, shard):
        shard = jnp.concatenate(self.from_z(shard), axis=0)
        for j in range(self.levels):
            shard = jnp.concatenate([shard, self.by_bit(shard, j)], axis=0)
        return shard, self.by_core(shard)

    def reduce(self, keep, send):
        keep, send = fold(keep, self.by_core(send), 2)
        for j in reversed(range(self.levels)):
            pieces = 2 if j else self.depth
            out = fold(keep, self.by_bit(send, j), pieces)
            keep, send = out[0], out[1]
        return self.exchange_z(out)

    def members(self):
        relative = jnp.arange(2 * self.depth, dtype=jnp.int32)
        core = self.core ^ (relative // self.depth)
        return core * self.depth + (self.z ^ (relative % self.depth))


def by_columns(width, step):
    chunk = 256 if width % 256 == 0 else 128
    if width % chunk or width <= 4 * chunk:
        step(slice(0, width))
        return

    def at(i, carry):
        step(pl.ds(pl.multiple_of(i * chunk, chunk), chunk))
        return carry

    lax.fori_loop(0, width // chunk, at, 0)


class Order:
    def __init__(self):
        self.last = ()

    def hold(self, array):
        return after(array, *self.last)

    def note(self, array):
        self.last = (array,)
        return array


def stack_rows(arrays):
    height = sum(a.shape[0] for a in arrays)
    if any(a.shape[0] % 8 for a in arrays):
        return jnp.concatenate(arrays, axis=0)

    def body(*refs):
        def copy(columns):
            at = 0
            for ref in refs[:-1]:
                refs[-1][at : at + ref.shape[0], columns] = ref[:, columns]
                at += ref.shape[0]

        by_columns(arrays[0].shape[1], copy)

    return run(body, "stack", [((height, arrays[0].shape[1]), arrays[0].dtype)], arrays)[0]


def after(array, *earlier):
    return lax.optimization_barrier((array, *earlier))[0]


def unit_rms(values):
    scale = lax.rsqrt(jnp.mean(values * values, -1, keepdims=True) + EPS)
    return values * scale, scale


def norm_back(grad, gain, unit, scale):
    scaled = grad * gain
    return scale * (scaled - unit * jnp.mean(scaled * unit, -1, keepdims=True))


def document_of(places, lengths):
    return (places >= lengths[0]).astype(jnp.int32)


def sigmoid(values):
    return 1.0 / (1.0 + jnp.exp(-values))


def soft(scores):
    top = jnp.max(scores, -1, keepdims=True)
    expo = jnp.exp(scores - top)
    return expo / jnp.sum(expo, -1, keepdims=True)


def two_parts(values):
    high = values.astype(BF16)
    return high, (values - high.astype(F32)).astype(BF16)


def place_rows(select, values):
    high, low = two_parts(values)
    return tn(select, high) + tn(select, low)


def take_rows(select, values):
    high, low = two_parts(values)
    return nn(select, high) + nn(select, low)


def reorder(values, order):
    high, low = two_parts(values)
    return nn(high, order) + nn(low, order)


def reorder_back(values, order):
    high, low = two_parts(values)
    return nt(high, order) + nt(low, order)


def into(values, first, second):
    half = first.shape[0]
    return nn(values[:, :half], first) + nn(values[:, half:], second)


def onto(values, first, second):
    return jnp.concatenate([nt(values, first), nt(values, second)], axis=1)


def lanes(rows, width=128):
    return lax.broadcasted_iota(jnp.int32, (rows, width), 1)


def both_heads(pair):
    first = lanes(pair.shape[0]) < HDL
    zero = jnp.zeros_like(pair)
    return jnp.concatenate([jnp.where(first, pair, zero), jnp.where(first, zero, pair)], axis=0)


def pair_at(p, start=0):
    return pl.ds(pl.multiple_of(start + p * 128, 128), 128)


def column_at(array, index):
    return jnp.sum(jnp.where(lanes(*array.shape) == index, array, 0.0), -1, keepdims=True)


def one_pair(stacked):
    rows = stacked.shape[0] // 2
    return jnp.where(lanes(rows) < HDL, stacked[:rows], stacked[rows:])


def run(body, name, outs, args, smem=0, scratch=(), room=ROOM):
    vmem = pl.BlockSpec(memory_space=pltpu.VMEM)
    held = sum(math.prod(piece.shape) * jnp.dtype(piece.dtype).itemsize for piece in scratch)
    cuts = {i: a for i, a in enumerate(args) if isinstance(a, Columns)}

    def kernel(*refs):
        refs = list(refs)
        for i, cut in cuts.items():
            refs[i] = refs[i].at[:, cut.start : cut.stop]
        body(*refs)

    return pl.pallas_call(
        kernel,
        name=name,
        compiler_params=pltpu.CompilerParams(vmem_limit_bytes=held + room),
        out_shape=[jax.ShapeDtypeStruct(shape, kind) for shape, kind in outs],
        in_specs=[pl.BlockSpec(memory_space=pltpu.SMEM)] * smem + [vmem] * (len(args) - smem),
        out_specs=[vmem] * len(outs),
        scratch_shapes=list(scratch),
        cost_estimate=declared(name),
    )(*[a.array if isinstance(a, Columns) else a for a in args])


def rearrange(name, sources, outs, room=ROOM):
    bounds = [b for unused, moves in outs for m in moves for b in (*m[1], m[3])]
    if any(b % 8 for b in bounds):
        made = []
        for shape, moves in outs:
            out = jnp.zeros(shape, BF16)
            for i, (r0, r1), (c0, c1), row, column in moves:
                out = lax.dynamic_update_slice(out, sources[i][r0:r1, c0:c1], (row, column))
            made.append(out)
        return made

    spans = {(c0, c1, column) for unused, moves in outs for i, rows, (c0, c1), row, column in moves}

    def body(*refs):
        def copy(columns=None):
            for out, (unused, moves) in zip(refs[len(sources) :], outs):
                for i, (r0, r1), (c0, c1), row, column in moves:
                    to = columns or slice(column, column + c1 - c0)
                    out[row : row + r1 - r0, to] = refs[i][r0:r1, columns or slice(c0, c1)]

        if len(spans) == 1 and all(c0 == column for c0, c1, column in spans):
            by_columns(max(c1 for c0, c1, column in spans), copy)
        else:
            copy()

    return run(body, name, [(shape, BF16) for shape, unused in outs], sources, room=room)


def fold(keep, moved, pieces, kind=BF16):
    height, width = keep.shape
    piece = height // pieces
    parts = 2 if piece % 32 == 0 else 1
    step = piece // parts

    def body(*refs):
        def add(columns):
            for k in range(pieces):
                total = refs[k][:, columns].astype(F32) + refs[pieces + k][:, columns].astype(F32)
                refs[2 * pieces + k][:, columns] = total.astype(kind)

        by_columns(width, add)

    def spec(k):
        return pl.BlockSpec((step, width), lambda i, k=k: (k * parts + i, 0))

    if piece % 8:
        total = keep.astype(F32) + moved.astype(F32)
        return [total[k * piece : (k + 1) * piece].astype(kind) for k in range(pieces)]
    return pl.pallas_call(
        body,
        name="fold",
        compiler_params=pltpu.CompilerParams(vmem_limit_bytes=ROOM),
        grid=(parts,),
        out_shape=[jax.ShapeDtypeStruct((piece, width), kind)] * pieces,
        in_specs=[spec(k) for k in range(pieces)] * 2,
        out_specs=[spec(0)] * pieces,
        cost_estimate=declared("fold"),
    )(*([keep] * pieces + [moved] * pieces))


def settle(pieces, widths, name, rows=None):
    rows = rows or pieces[0].shape[0]

    def body(*refs):
        parts, outs = refs[: len(pieces)], refs[len(pieces) :]
        at = 0
        for out, width in zip(outs, widths):
            total = parts[0][:rows, at : at + width].astype(F32)
            for part in parts[1:]:
                total = total + part[:rows, at : at + width].astype(F32)
            out[...] = total
            at += width

    return run(body, name, [((rows, width), F32) for width in widths], pieces)


def hot(column, rows):
    return jnp.where(column == lanes(column.shape[0], rows), 1.0, 0.0).astype(BF16)


def as_column(row):
    count = row.shape[1]
    eye = lax.broadcasted_iota(jnp.int32, (count, count), 0) == lanes(count, count)
    spread = jnp.where(eye, row.astype(F32), 0.0)
    return jnp.sum(spread, -1, keepdims=True).astype(jnp.int32)


def order_matrix(order):
    width = order.shape[1]
    rows = lax.broadcasted_iota(jnp.int32, (width, width), 0)
    return jnp.where(rows == order, 1.0, 0.0).astype(BF16)


def orders_body(orders, to_own, to_slice):
    to_own[...] = order_matrix(orders[0:1])
    to_slice[...] = order_matrix(orders[1:2])


def select_body(
    place, to_own, query_route, key_route, feed_route, cotangent, cot, query_select, key_select, feed_select, query_doc
):
    rows = cotangent.shape[0]
    cot[...] = nn(cotangent[...], to_own[...]).astype(BF16)
    queries = as_column(query_route[pl.ds(place[4], 1)])
    query_select[...] = hot(queries, rows)
    key_select[...] = hot(as_column(key_route[pl.ds(place[4], 1)]), rows)
    feed_select[...] = hot(as_column(feed_route[...]), rows)
    query_doc[...] = jnp.where(place[0] + queries >= place[1], 1, 0)


def pack_body(
    place, key_spots, tokens, key_route, q_l, k_l, v_l,
    gate_s, up_s, down_s, gate_l, up_l, down_l, second, third, expert_keep, expert_send, key_docs
):
    part, width = q_l.shape
    at = 0
    for ref in (q_l, k_l, v_l):
        second[:, at : at + ref.shape[1]] = ref[...]
        at += ref.shape[1]
    keyed = nn(hot(as_column(key_route[pl.ds(place[4], 1)]), tokens.shape[0]), tokens[...])
    second[:, at : at + width] = keyed[:part].astype(BF16)
    rest = keyed[part:]
    chunk = width * rest.shape[0] // part
    pieces = [rest[:, i * chunk : (i + 1) * chunk] for i in range(width // chunk)]
    second[:, at + width :] = jnp.concatenate(pieces, axis=0).astype(BF16)
    narrow = gate_s.shape[1]
    for i, ref in enumerate((gate_s, up_s, down_s)):
        third[:, i * narrow : (i + 1) * narrow] = ref[...]
    share = expert_keep.shape[1] // 3
    depth = expert_keep.shape[0] // part
    for c, expert in enumerate((expert_keep, expert_send)):
        for k in range(depth):
            at = ((place[5] ^ c) * depth + (place[6] ^ k)) * share
            at = pl.ds(pl.multiple_of(at, share), share)
            for i, ref in enumerate((gate_l, up_l, down_l)):
                expert[k * part : (k + 1) * part, i * share : (i + 1) * share] = ref[:, at]
    blocks, slots = key_route.shape
    keys = key_spots.shape[1]
    block = lax.broadcasted_iota(jnp.int32, (blocks, keys), 0) == key_spots[0:1]
    table = key_route[...].astype(F32).T.astype(BF16)
    found = nn(table, jnp.where(block, 1.0, 0.0).astype(BF16))
    slot = lax.broadcasted_iota(jnp.int32, (slots, keys), 0) == key_spots[1:2]
    position = jnp.sum(jnp.where(slot, found, 0.0), 0, keepdims=True).astype(jnp.int32)
    rows = tokens.shape[0]
    document = jnp.where(key_spots[0:1] * rows + position >= place[1], 1, 0)
    key_docs[...] = jnp.where(position < rows, document, -1)


def prepare_body(to_own, above, tokens, below, raw):
    order = to_own[...]
    at = 0
    for ref in (above, tokens, below):
        raw[at : at + ref.shape[0]] = nn(ref[...], order).astype(BF16)
        at += ref.shape[0]


def unpack_body(place, keep, got, gate, up, down):
    part = gate.shape[0]
    depth = keep.shape[0] // part
    share = keep.shape[1] // 3
    for c, source in enumerate((keep, got)):
        for k in range(depth):
            at = ((place[5] ^ c) * depth + (place[6] ^ k)) * share
            at = pl.ds(pl.multiple_of(at, share), share)
            for i, out in enumerate((gate, up, down)):
                piece = source[k * part : (k + 1) * part, i * share : (i + 1) * share]
                out[:, at] = piece.astype(F32)


def pair_up(shard, first, second, part):
    count = first.shape[0] // part
    width = first.shape[1]
    whole, own = (0, part), (0, width)
    outs = []
    for k in range(count):
        at = (k * part, (k + 1) * part)
        moves = [(0, whole, (0, 2 * width), 0, 0), (1, at, own, part, 0), (2, at, own, part, width)]
        outs.append(((2 * part, 2 * width), moves))
    return rearrange("pair_up", (shard, first, second), outs)


def stack_both(pieces, name="stack_both"):
    height = sum(p.shape[0] for p in pieces)
    width = pieces[0].shape[1]
    moves, row = [], 0
    for i, piece in enumerate(pieces):
        n = piece.shape[0] // 2
        moves.append((i, (0, n), (0, width), row, 0))
        moves.append((i, (n, 2 * n), (0, width), height // 2 + row, 0))
        row += n
    return rearrange(name, pieces, [((height, width), moves)])[0]


def part_both(pieces, name):
    height = sum(p.shape[0] for p in pieces) // 2
    width = pieces[0].shape[1]
    first, second, row = [], [], 0
    for i, piece in enumerate(pieces):
        n = piece.shape[0] // 2
        first.append((i, (0, n), (0, width), row, 0))
        second.append((i, (n, 2 * n), (0, width), row, 0))
        row += n
    return rearrange(name, pieces, [((height, width), first), ((height, width), second)])


def take_apart(pieces, part):
    width = pieces[0].shape[1] // 2
    outs = []
    for side in range(2):
        columns = (side * width, (side + 1) * width)
        moves = [(k, (0, part), columns, k * part, 0) for k in range(len(pieces))]
        outs.append(((len(pieces) * part, width), moves))
    return rearrange("take_apart", pieces, outs)


def local_mask(place, tile, reach, stacked, span):
    shape = (stacked, span)
    row = lax.broadcasted_iota(jnp.int32, shape, 0) & (reach - 1)
    query = place[0] + tile * reach + row
    key = place[0] + (tile - 1) * reach + lax.broadcasted_iota(jnp.int32, shape, 1)
    split, live, total = place[1], place[1] + place[2], place[3]
    inside = (key >= 0) & (key < total)
    same = jnp.where(query >= split, 1, 0) == jnp.where(key >= split, 1, 0)
    near = jnp.abs(query - key) <= reach
    both = ((query < live) & (key < live)) | (query == key)
    return near & inside & same & both


def light_rows_body(raw, w0, w1, normed, queries, pairs, vectors):
    light = HL * HDL
    reach = RADIUS
    rows = queries.shape[0]
    columns = [w[:, 3 * light :].astype(F32).T[:8] for w in (w0, w1)]
    vectors[...] = jnp.concatenate(columns, axis=1)
    unit, unused = unit_rms(raw[...].astype(F32))
    normed[...] = (unit * vectors[0:1]).astype(BF16)
    own = normed[reach : reach + rows]
    queries[...] = into(own, w0[:, :light], w1[:, :light]).astype(BF16)
    pairs[...] = into(normed[...], w0[:, light : 3 * light], w1[:, light : 3 * light]).astype(BF16)


def light_forward_body(place, queries, pairs, mixed, sums):
    light = HL * HDL
    reach = RADIUS
    rows = queries.shape[0]
    scale = 1.0 / math.sqrt(HDL)
    lane = lanes(reach)
    for tile in range(rows // reach):
        mine = slice(tile * reach, (tile + 1) * reach)
        seen = slice(tile * reach, (tile + 3) * reach)
        mask = local_mask(place, tile, reach, 2 * reach, 3 * reach)

        def pair(p, logs):
            query = both_heads(queries[mine, pair_at(p)])
            scores = jnp.where(mask, nt(query, pairs[seen, pair_at(p)]) * scale, NEG)
            top = jnp.max(scores, -1, keepdims=True)
            expo = jnp.exp(scores - top)
            total = jnp.sum(expo, -1, keepdims=True)
            probs = (expo * (1.0 / total)).astype(BF16)
            mixed[mine, pair_at(p)] = one_pair(nn(probs, pairs[seen, pair_at(p, light)])).astype(BF16)
            log = top + jnp.log(total)
            logs = jnp.where(lane == 2 * p, log[:reach], logs)
            return jnp.where(lane == 2 * p + 1, log[reach:], logs)

        logs = lax.fori_loop(0, HL // 2, pair, jnp.zeros((reach, 128), F32))
        sums[mine] = logs


def piece_select(block_rows, rest, part, piece):
    shape = (block_rows // part * rest, block_rows)
    k = lax.broadcasted_iota(jnp.int32, shape, 0)
    row = lax.broadcasted_iota(jnp.int32, shape, 1)
    shift = rest.bit_length() - 1
    want = (k >> shift) * part + piece * rest + (k & (rest - 1))
    return jnp.where(row == want, 1.0, 0.0).astype(BF16)


def heavy_rows_body(slots, vectors, to_own, s0, s1, keyed, held):
    width = to_own.shape[0]
    half = s0.shape[0]
    at = 3 * HH * HDH
    part = half // (keyed.shape[0] // slots // 2)
    rest = slots - part
    chunk = width * rest // part
    for i, ref in enumerate((s0, s1)):
        held[i * half : (i + 1) * half] = ref[:, at : at + width]
        low = 2 * half + i * (half // part * rest)
        for piece in range(part // rest):
            picked = nn(piece_select(half, rest, part, piece), ref[:, at + width :])
            held[low : low + half // part * rest, piece * chunk : (piece + 1) * chunk] = picked.astype(BF16)
    step = 256

    def project(t, carry):
        rows = pl.ds(pl.multiple_of(t * step, step), step)
        unit, unused = unit_rms(nn(held[rows], to_own[...]))
        keyed[rows] = (unit * vectors[0:1]).astype(BF16)
        return carry

    lax.fori_loop(0, keyed.shape[0] // step, project, 0)


def heavy_pairs_body(select, normed, keyed, s0, s1, pairs, routed, queries):
    heavy = HH * HDH
    q_at = slice(0, heavy)
    kv_at = slice(heavy, 3 * heavy)
    step = 256

    def project(t, carry):
        rows = pl.ds(pl.multiple_of(t * step, step), step)
        pairs[rows] = into(keyed[rows], s0[:, kv_at], s1[:, kv_at]).astype(BF16)
        return carry

    lax.fori_loop(0, keyed.shape[0] // step, project, 0)
    own = normed[RADIUS : normed.shape[0] - RADIUS]
    routed[...] = nn(select[...], own).astype(BF16)
    queries[...] = into(routed[...], s0[:, q_at], s1[:, q_at]).astype(BF16)


def heavy_forward_body(query_doc, key_doc, queries, pairs, mixed, sums):
    heavy = HH * HDH
    slots = queries.shape[0]
    scale = 1.0 / math.sqrt(HDH)
    mask = jnp.concatenate([query_doc[...], query_doc[...]], axis=0) == key_doc[...]

    def pair(p, logs):
        scores = jnp.where(mask, nt(both_heads(queries[:, pair_at(p)]), pairs[:, pair_at(p)]) * scale, NEG)
        top = jnp.max(scores, -1, keepdims=True)
        expo = jnp.exp(scores - top)
        total = jnp.sum(expo, -1, keepdims=True)
        probs = (expo * (1.0 / total)).astype(BF16)
        mixed[:, pair_at(p)] = one_pair(nn(probs, pairs[:, pair_at(p, heavy)])).astype(BF16)
        return jnp.where(lanes(2 * slots) == p, top + jnp.log(total), logs)

    logs = lax.fori_loop(0, HH // 2, pair, jnp.zeros((2 * slots, 128), F32))
    sums[...] = logs


def join_body(
    raw, light_mixed, heavy_mixed, routed, query_select, feed_select, vectors, cot, to_own, s0, s1,
    middle, normed, heavy_branch, feed_rows, feed_grads, sent
):
    heavy = HH * HDH
    width = raw.shape[1]
    rows = middle.shape[0]
    at = slice(heavy, heavy + HL * HDL)
    light_branch = onto(light_mixed[...], s0[:, at], s1[:, at])
    at = slice(0, heavy)
    heavy_branch[...] = onto(heavy_mixed[...], s0[:, at], s1[:, at])
    score = sigmoid(jnp.sum(routed[...].astype(F32) * vectors[1:2], -1, keepdims=True))
    inputs = raw[RADIUS : RADIUS + rows].astype(F32)
    middle[...] = inputs + light_branch + place_rows(query_select[...], score * heavy_branch[...])
    unit, unused = unit_rms(middle[...])
    normed[...] = (unit * vectors[2:3]).astype(BF16)
    feed_rows[...] = nn(feed_select[...], normed[...]).astype(BF16)
    feed_grads[...] = nn(feed_select[...], cot[...])
    score = sigmoid(jnp.sum(feed_rows[...].astype(F32) * vectors[3:4], -1, keepdims=True))
    sent[:, :width] = nt(feed_rows[...], to_own[...]).astype(BF16)
    sent[:, width:] = nt((score * feed_grads[...]).astype(BF16), to_own[...]).astype(BF16)


def geglu_rows(gate, upper, grad_hidden):
    c0, c1 = 0.7978845608028654, 0.044715
    square = gate * gate
    bent = jnp.tanh(c0 * gate * (1.0 + c1 * square))
    bell = 0.5 * (1.0 + bent)
    gelu = gate * bell
    slope = bell + 0.5 * gate * (1.0 - bent * bent) * (c0 * (1.0 + 3.0 * c1 * square))
    return gelu * upper, grad_hidden * upper * slope, grad_hidden * gelu


def geglu_loop(wide, grad_hidden, hidden, grads):
    count = hidden.shape[1]
    step = 32

    def rows_at(t, carry):
        rows = pl.ds(pl.multiple_of(t * step, step), step)
        out, grad_gate, grad_upper = geglu_rows(
            wide[rows, :count], wide[rows, count:], grad_hidden[rows]
        )
        hidden[rows] = out.astype(BF16)
        grads[rows, :count] = grad_gate.astype(BF16)
        grads[rows, count:] = grad_upper.astype(BF16)
        return carry

    lax.fori_loop(0, hidden.shape[0] // step, rows_at, 0)


def feed_body(normed, cot, t0, t1, feed, grad_normed, hidden, grads, wide, grad_hidden):
    narrow = hidden.shape[1]
    wide[...] = into(normed[...], t0[:, : 2 * narrow], t1[:, : 2 * narrow])
    grad_hidden[...] = into(cot[...], t0[:, 2 * narrow :], t1[:, 2 * narrow :])
    geglu_loop(wide, grad_hidden, hidden, grads)
    feed[...] = onto(hidden[...], t0[:, 2 * narrow :], t1[:, 2 * narrow :])
    grad_normed[...] = onto(grads[...], t0[:, : 2 * narrow], t1[:, : 2 * narrow])


def feed_weight_body(normed, cot, hidden, grads, keep, send):
    narrow = hidden.shape[1]
    half = keep.shape[0]
    for out, at in ((send, slice(half, None)), (keep, slice(0, half))):
        out[:, : 2 * narrow] = tn(normed[:, at], grads[...]).astype(out.dtype)
        out[:, 2 * narrow :] = tn(cot[:, at], hidden[...]).astype(out.dtype)


def expert_body(got0, got1, to_slice, weights, keep, send, grad_keep, grad_send, rows, row_grads, wide, grad_hidden, hidden, grads):
    width = to_slice.shape[0]
    share = hidden.shape[1]
    count = got0.shape[0]
    for i, got in enumerate((got0, got1)):
        at = slice(i * count, (i + 1) * count)
        rows[at] = nn(got[:, :width], to_slice[...]).astype(BF16)
        row_grads[at] = nn(got[:, width:], to_slice[...]).astype(BF16)
    first, second = weights[:, : 2 * share], weights[:, 3 * share : 5 * share]
    first_down, second_down = weights[:, 2 * share : 3 * share], weights[:, 5 * share :]
    wide[...] = into(rows[...], first, second)
    grad_hidden[...] = into(row_grads[...], first_down, second_down)
    geglu_loop(wide, grad_hidden, hidden, grads)
    for out, at in ((send, slice(count, None)), (keep, slice(0, count))):
        feed = onto(hidden[at], first_down, second_down).astype(BF16)
        back = onto(grads[at], first, second).astype(BF16)
        out[:, :width] = nt(feed, to_slice[...]).astype(out.dtype)
        out[:, width:] = nt(back, to_slice[...]).astype(out.dtype)
    half = weights.shape[0]
    low = grad_keep.shape[0]
    for i in range(2):
        at = slice(i * half, (i + 1) * half)
        to = 3 * share * i
        for left, right, columns in (
            (rows, grads, slice(to, to + 2 * share)), (row_grads, hidden, slice(to + 2 * share, to + 3 * share))
        ):
            product = tn(left[:, at], right[...]).astype(BF16)
            grad_keep[:, columns] = product[:low]
            grad_send[:, columns] = product[low:]


def turn_body(*refs):
    pieces = refs[:-12]
    (
        middle, feed, grad_normed, feed_rows, feed_grads, feed_select, vectors, cot, to_own,
        result, grad_middle, vector_grads,
    ) = refs[-12:]
    width = middle.shape[1]
    summed = pieces[0][...].astype(F32)
    for piece in pieces[1:]:
        summed = summed + piece[...].astype(F32)
    feed_heavy = reorder(summed[:, :width], to_own[...])
    grad_rows = reorder(summed[:, width:], to_own[...])
    rows = feed_rows[...].astype(F32)
    score = sigmoid(jnp.sum(rows * vectors[3:4], -1, keepdims=True))
    logit = jnp.sum(feed_grads[...] * feed_heavy, -1, keepdims=True) * score * (1.0 - score)
    grad_rows = grad_rows + logit * vectors[3:4]
    grads = grad_normed[...] + place_rows(feed_select[...], grad_rows)
    unit, scale = unit_rms(middle[...])
    grad_middle[...] = cot[...].astype(F32) + norm_back(grads, vectors[2:3], unit, scale)
    vector_grads[...] = jnp.concatenate(
        [
            jnp.zeros((2, width), F32),
            jnp.sum(grads * unit, 0, keepdims=True),
            jnp.sum(rows * logit, 0, keepdims=True),
            jnp.zeros((4, width), F32),
        ],
        axis=0,
    )
    out = middle[...] + feed[...] + place_rows(feed_select[...], score * feed_heavy)
    result[...] = nt(out.astype(BF16), to_own[...]).astype(BF16)


def heavy_scores_body(
    query_doc, key_doc, grad_middle, query_select, routed, pairs, queries, heavy_branch, sums, vectors, s0, s1,
    grad_branch, grad_queries, grad_pairs, logits, held
):
    heavy = HH * HDH
    score = sigmoid(jnp.sum(routed[...].astype(F32) * vectors[1:2], -1, keepdims=True))
    grad_rows = take_rows(query_select[...], grad_middle[...])
    grad_branch[...] = (score * grad_rows).astype(BF16)
    logit = jnp.sum(grad_rows * heavy_branch[...], -1, keepdims=True) * score * (1.0 - score)
    logits[...] = jnp.broadcast_to(logit, logits.shape)
    at = slice(0, heavy)
    grad_mixed = into(grad_branch[...], s0[:, at], s1[:, at]).astype(BF16)
    scale = 1.0 / math.sqrt(HDH)
    mask = jnp.concatenate([query_doc[...], query_doc[...]], axis=0) == key_doc[...]
    held[...] = grad_mixed
    logs = sums[...]

    def pair(p, carry):
        query = both_heads(queries[:, pair_at(p)])
        grad_out = both_heads(held[:, pair_at(p)])
        key = pairs[:, pair_at(p)]
        scores = jnp.where(mask, nt(query, key) * scale, NEG)
        probs = jnp.exp(scores - column_at(logs, p))
        grad_probs = nt(grad_out, pairs[:, pair_at(p, heavy)])
        delta = jnp.sum(probs * grad_probs, -1, keepdims=True)
        grad_scores = (probs * (grad_probs - delta)).astype(BF16)
        grad_queries[:, pair_at(p)] = one_pair(nn(grad_scores, key) * scale).astype(BF16)
        grad_pairs[:, pair_at(p)] = (tn(grad_scores, query) * scale).astype(BF16)
        grad_pairs[:, pair_at(p, heavy)] = tn(probs.astype(BF16), grad_out).astype(BF16)
        return carry

    lax.fori_loop(0, HH // 2, pair, 0)


def heavy_weights_body(
    grad_middle, routed, keyed, light_mixed, heavy_mixed, grad_branch, grad_queries, grad_pairs, logits, vectors, to_own, s0, s1,
    keep, send, vector_grads, moved
):
    width = grad_middle.shape[1]
    heavy = HH * HDH
    light = HL * HDL
    half = s0.shape[0]
    slots = routed.shape[0]
    q_at = slice(width + light, width + light + heavy)
    kv_at = slice(width + light + heavy, width + light + 3 * heavy)
    logit = logits[:, 0:1]
    step = 256

    def back(t, gain):
        rows = pl.ds(pl.multiple_of(t * step, step), step)
        grads = onto(grad_pairs[rows], s0[:, heavy : 3 * heavy], s1[:, heavy : 3 * heavy])
        moved[rows] = nt(grads.astype(BF16), to_own[...]).astype(BF16)
        return gain + jnp.sum(grads * keyed[rows].astype(F32), 0, keepdims=True)

    gain = lax.fori_loop(0, keyed.shape[0] // step, back, jnp.zeros((1, width), F32))
    vector_grads[...] = jnp.concatenate(
        [
            gain / vectors[0:1],
            jnp.sum(routed[...].astype(F32) * logit, 0, keepdims=True),
            jnp.zeros((6, width), F32),
        ],
        axis=0,
    )
    low = grad_middle[...].astype(BF16)
    part = half // (keyed.shape[0] // slots // 2)
    rest = slots - part
    chunk = width * rest // part
    for i, out in ((1, send), (0, keep)):
        at = slice(i * half, (i + 1) * half)
        out[:, :width] = tn(grad_branch[:, at], heavy_mixed[...]).astype(BF16)
        out[:, width : width + light] = tn(low[:, at], light_mixed[...]).astype(BF16)
        out[:, q_at] = tn(routed[:, at], grad_queries[...]).astype(BF16)
        out[:, kv_at] = tn(keyed[:, at], grad_pairs[...]).astype(BF16)
        to = width + light + 3 * heavy
        out[:, to : to + width] = moved[at]
        at = 2 * half + i * (half // part * rest)
        total = 0.0
        for piece in range(part // rest):
            block = moved[at : at + half // part * rest, piece * chunk : (piece + 1) * chunk]
            total = total + tn(piece_select(half, rest, part, piece), block)
        out[:, to + width :] = total.astype(BF16)


def routed_body(grad_queries, logits, vectors, s0, s1, grad_routed):
    at = slice(0, HH * HDH)
    grad_routed[...] = onto(grad_queries[...], s0[:, at], s1[:, at]) + logits[:, 0:1] * vectors[1:2]


def light_scores_body(place, grad_middle, queries, pairs, sums, s0, s1, grad_queries, grad_pairs, held, grad_out_all):
    light = HL * HDL
    heavy = HH * HDH
    reach = RADIUS
    rows = queries.shape[0]
    at = slice(heavy, heavy + light)
    grad_out_all[...] = into(grad_middle[...].astype(BF16), s0[:, at], s1[:, at]).astype(BF16)
    held[...] = jnp.zeros_like(held)
    scale = 1.0 / math.sqrt(HDL)
    for tile in range(rows // reach):
        mine = slice(tile * reach, (tile + 1) * reach)
        seen = slice(tile * reach, (tile + 3) * reach)
        mask = local_mask(place, tile, reach, 2 * reach, 3 * reach)
        logs = sums[mine]

        def pair(p, carry):
            query = both_heads(queries[mine, pair_at(p)])
            grad_out = both_heads(grad_out_all[mine, pair_at(p)])
            key = pairs[seen, pair_at(p)]
            log = jnp.concatenate([column_at(logs, 2 * p), column_at(logs, 2 * p + 1)], axis=0)
            probs = jnp.exp(jnp.where(mask, nt(query, key) * scale, NEG) - log)
            grad_probs = nt(grad_out, pairs[seen, pair_at(p, light)])
            delta = jnp.sum(probs * grad_probs, -1, keepdims=True)
            grad_scores = (probs * (grad_probs - delta)).astype(BF16)
            grad_queries[mine, pair_at(p)] = one_pair(nn(grad_scores, key) * scale).astype(BF16)
            held[seen, pair_at(p)] = held[seen, pair_at(p)] + tn(grad_scores, query) * scale
            beyond = pair_at(p, light)
            held[seen, beyond] = held[seen, beyond] + tn(probs.astype(BF16), grad_out)
            return carry

        lax.fori_loop(0, HL // 2, pair, 0)
    grad_pairs[...] = held[...].astype(BF16)


def light_weights_body(
    raw, normed, grad_queries, grad_pairs, grad_routed, query_select, feed_vectors, heavy_vectors, to_own, f0, f1,
    keep, send, outer, grad_mine
):
    light = HL * HDL
    reach = RADIUS
    rows = grad_queries.shape[0]
    half = f0.shape[0]
    grads = onto(grad_pairs[...], f0[:, light : 3 * light], f1[:, light : 3 * light])
    for i, at in enumerate((slice(0, reach), slice(reach + rows, None))):
        outer[i * reach : (i + 1) * reach] = nt(grads[at].astype(BF16), to_own[...]).astype(BF16)
    own = onto(grad_queries[...], f0[:, :light], f1[:, :light])
    own = own + grads[reach : reach + rows] + place_rows(query_select[...], grad_routed[...])
    grad_mine[...] = own
    unit, unused = unit_rms(raw[...].astype(F32))
    gain = jnp.sum(own * unit[reach : reach + rows], 0, keepdims=True)
    for at in (slice(0, reach), slice(reach + rows, None)):
        gain = gain + jnp.sum(grads[at] * unit[at], 0, keepdims=True)
    vector_rows = feed_vectors[...] + heavy_vectors[...]
    first = lax.broadcasted_iota(jnp.int32, vector_rows.shape, 0) == 0
    vector_rows = vector_rows + jnp.where(first, gain, 0.0)
    filler = jnp.zeros((120, raw.shape[1]), F32)
    columns = jnp.concatenate([vector_rows, filler], axis=0)
    for i, out in ((1, send), (0, keep)):
        at = slice(i * half, (i + 1) * half)
        out[:, :light] = tn(normed[reach : reach + rows, at], grad_queries[...]).astype(BF16)
        out[:, light : 3 * light] = tn(normed[:, at], grad_pairs[...]).astype(BF16)
        out[:, 3 * light :] = columns[:, at].T.astype(BF16)


def halo_body(from_prev, from_next, grad_mine, to_own, out):
    reach = RADIUS
    rows = grad_mine.shape[0]
    order = to_own[...]
    out[...] = grad_mine[...]
    out[:reach] = out[:reach] + nn(from_prev[...], order)
    out[rows - reach :] = out[rows - reach :] + nn(from_next[...], order)


def finish_body(keyed_grads, key_select, grads, grad_middle, raw, vectors, to_own, out):
    reach = RADIUS
    rows, width = grads.shape
    order = to_own[...]
    keyed = keyed_grads[...]
    if keyed.shape[0] < key_select.shape[0]:
        rest = key_select.shape[0] - keyed.shape[0]
        tail = [keyed[i * rest : (i + 1) * rest, width:] for i in range(keyed.shape[0] // rest)]
        keyed = jnp.concatenate([keyed[:, :width], jnp.concatenate(tail, axis=1)], axis=0)
    keyed = nn(keyed.astype(BF16), order).astype(BF16)
    total = grads[...] + tn(key_select[...], keyed)
    unit, scale = unit_rms(raw[reach : reach + rows].astype(F32))
    total = grad_middle[...] + norm_back(total, vectors[0:1], unit, scale)
    out[...] = reorder_back(total, order)


def heavy_forward_wide(query_doc, key_doc, select, normed, vectors, to_own, s0, s1, keyed_raw):
    heavy = HH * HDH
    q_at, kv_at = slice(0, heavy), slice(heavy, 3 * heavy)
    unit, unused = unit_rms(nn(keyed_raw, to_own))
    keyed = (unit * vectors[0:1]).astype(BF16)
    pairs = into(keyed, s0[:, kv_at], s1[:, kv_at]).astype(BF16)
    routed = nn(select, normed[RADIUS : normed.shape[0] - RADIUS]).astype(BF16)
    queries = into(routed, s0[:, q_at], s1[:, q_at]).astype(BF16)

    def heads(array):
        return array.reshape(-1, HH, HDH)

    scores = jnp.einsum(
        "qhd,khd->hqk", heads(queries), heads(pairs[:, :heavy]), preferred_element_type=F32
    ) / math.sqrt(HDH)
    probs = soft(jnp.where((query_doc == key_doc)[None], scores, NEG))
    mixed = jnp.einsum(
        "hqk,khd->qhd", probs.astype(BF16), heads(pairs[:, heavy:]), preferred_element_type=F32
    )
    return keyed, pairs, routed, queries, mixed.reshape(-1, heavy).astype(BF16), probs


def heavy_backward_wide(
    grad_middle, query_select, routed, keyed, pairs, queries, light_mixed, heavy_mixed, heavy_branch, probs,
    vectors, to_own, o0, o1, s0, s1
):
    heavy = HH * HDH
    scale = 1.0 / math.sqrt(HDH)
    half = s0.shape[0]
    q_at, kv_at = slice(0, heavy), slice(heavy, 3 * heavy)
    score = sigmoid(jnp.sum(routed.astype(F32) * vectors[1:2], -1, keepdims=True))
    grad_rows = take_rows(query_select, grad_middle)
    grad_branch = (score * grad_rows).astype(BF16)
    logit = jnp.sum(grad_rows * heavy_branch, -1, keepdims=True) * score * (1.0 - score)
    at = slice(0, heavy)
    grad_mixed = into(grad_branch, o0[:, at], o1[:, at]).astype(BF16)

    def heads(array):
        return array.reshape(-1, HH, HDH)

    def mix(pattern, left, right):
        return jnp.einsum(pattern, left, right, preferred_element_type=F32)

    grad_probs = mix("qhd,khd->hqk", heads(grad_mixed), heads(pairs[:, heavy:]))
    delta = jnp.sum(probs * grad_probs, -1, keepdims=True)
    grad_scores = (probs * (grad_probs - delta)).astype(BF16)
    grad_queries = mix("hqk,khd->qhd", grad_scores, heads(pairs[:, :heavy])) * scale
    grad_queries = grad_queries.reshape(-1, heavy).astype(BF16)
    grad_keys = mix("hqk,qhd->khd", grad_scores, heads(queries)) * scale
    grad_values = mix("hqk,qhd->khd", probs.astype(BF16), heads(grad_mixed))
    grad_pairs = jnp.concatenate(
        [grad_keys.reshape(-1, heavy).astype(BF16), grad_values.reshape(-1, heavy).astype(BF16)], axis=1
    )
    grad_routed = onto(grad_queries, s0[:, q_at], s1[:, q_at]) + logit * vectors[1:2]
    grads = onto(grad_pairs, s0[:, kv_at], s1[:, kv_at])
    vector_grads = jnp.concatenate(
        [
            jnp.sum(grads * keyed.astype(F32), 0, keepdims=True) / vectors[0:1],
            jnp.sum(routed.astype(F32) * logit, 0, keepdims=True),
            jnp.zeros((6, grads.shape[1]), F32),
        ],
        axis=0,
    )
    moved = nt(grads.astype(BF16), to_own).astype(BF16)
    low = grad_middle.astype(BF16)
    sides = []
    for at in (slice(0, half), slice(half, None)):
        columns = (
            tn(grad_branch[:, at], heavy_mixed),
            tn(low[:, at], light_mixed),
            tn(routed[:, at], grad_queries),
            tn(keyed[:, at], grad_pairs),
        )
        sides.append(jnp.concatenate(columns, axis=1).astype(BF16))
    return sides[0], sides[1], grad_routed, vector_grads, moved


def per_device(
    tokens,
    query_small,
    key_small,
    value_small,
    out_small,
    query_large,
    key_large,
    value_large,
    out_large,
    attend_gain,
    attend_router,
    gate_small,
    up_small,
    down_small,
    gate_large,
    up_large,
    down_large,
    feed_gain,
    feed_router,
    lengths,
    query_route,
    key_route,
    feed_route,
    cotangent,
):
    net = Net()
    rows, width = tokens.shape
    blocks = net.count
    part = width // blocks
    half = width // 2
    first = net.device * rows
    light = HL * HDL
    heavy = HH * HDH
    narrow = down_small.shape[0]
    wide = down_large.shape[0]
    slots = query_route.shape[1]
    members = 2 * net.depth
    share = wide // members
    pooled = members * slots
    keys = blocks * slots
    rest = slots - part
    packed = part % 8 == 0 and rest > 0 and rest % 8 == 0 and part % rest == 0 and keys <= 2048

    step = [(i, i + 1) for i in range(blocks - 1)]
    back = [(i + 1, i) for i in range(blocks - 1)]
    vector_pack = jnp.stack([attend_gain, attend_router, feed_gain, feed_router], axis=1)
    vector_pack = jnp.pad(vector_pack, ((0, 0), (0, 124)))
    first_pack = (query_small, key_small, value_small, vector_pack, out_large.T, out_small.T)
    moves, at = [], 0
    for i, piece in enumerate(first_pack):
        moves.append((i, (0, part), (0, piece.shape[1]), 0, at))
        at += piece.shape[1]
    (first_set,) = rearrange("pack_first", first_pack, [((part, at), moves)], room=56 << 20)
    first_parts = net.from_z(first_set)
    cut = 3 * light + vector_pack.shape[1]
    column = jnp.arange(width, dtype=jnp.int32)
    own_order = net.target(column // part) * part + column % part
    bits = column % half // (part * net.depth)
    bits = jnp.where(net.core == 1, bits, reverse_bits(bits, net.levels))
    member = (net.core ^ (column // half)) * net.depth + (net.z ^ (column // part % net.depth))
    slice_order = ((net.pair ^ bits) * members + member) * part + column % part
    orders = jnp.stack([own_order, slice_order])
    place = jnp.stack([first, lengths[0], lengths[1], jnp.int32(rows * blocks), net.device, net.core, net.z])
    square = ((width, width), BF16)
    chosen = ((slots, rows), BF16)

    if packed:
        tall = blocks * part
        spot = jnp.arange(keys, dtype=jnp.int32)
        spot_block = jnp.where(spot < tall, spot // part, (spot - tall) // rest)
        spot_slot = jnp.where(spot < tall, spot % part, part + (spot - tall) % rest)
        second_set, third_set, slices_keep, slices_send, key_docs = run(
            pack_body,
            "pack",
            [
                ((part, 4 * width + width * rest // part), BF16),
                ((part, 3 * narrow), BF16),
                ((net.depth * part, 3 * share), BF16),
                ((net.depth * part, 3 * share), BF16),
                ((1, keys), jnp.int32),
            ],
            (
                place, jnp.stack([net.target(spot_block), spot_slot]), tokens, key_route,
                query_large, key_large, value_large,
                gate_small, up_small, down_small.T, gate_large, up_large, down_large.T,
            ),
            smem=1,
            room=56 << 20,
        )
    else:
        second_set = jnp.concatenate([query_large, key_large, value_large], axis=1)
        third_set = jnp.concatenate([gate_small, up_small, down_small.T], axis=1)
        stacked = jnp.stack([gate_large, up_large, down_large.T], axis=0)
        stacked = stacked.reshape(3, part, members, share).transpose(2, 1, 0, 3)
        stacked = jnp.take(stacked.reshape(members, part, 3 * share), net.members(), axis=0)
        slices_keep, slices_send = stacked.reshape(2, net.depth * part, 3 * share)
    order = Order()
    top_bit = net.levels - 1

    def take_z(pieces):
        return order.note(stack_rows([order.hold(pieces[0])] + pieces[1:]))

    def take(whole, moved):
        return order.note(stack_rows([whole, order.hold(moved)]))

    def first_moved(whole):
        return net.by_bit(whole, 0)

    def rest_moved(whole, moved):
        for j in range(1, net.levels):
            whole = take(whole, moved)
            moved = net.by_bit(whole, j)
        return whole, moved

    order.note(second_set)
    first_set = take_z(first_parts)
    first_moving = first_moved(first_set)
    second_parts = net.from_z(after(second_set, first_set))
    slices_got = net.by_core(slices_send)
    to_own, to_slice = run(orders_body, "orders", [square, square], (order.hold(orders),))
    order.note(to_own)
    third_parts = pair_up(third_set, order.hold(slices_keep), slices_got, part)
    order.note(third_parts[0])
    first_set, first_moving = rest_moved(first_set, first_moving)
    second_set = take_z(second_parts)
    third_parts = net.exchange_z([after(p, second_set) for p in third_parts])
    cot, query_select, key_select, feed_select, query_docs = run(
        select_body,
        "select",
        [((rows, width), BF16), chosen, chosen, chosen, ((slots, 1), jnp.int32)],
        (place, to_own, query_route, key_route, feed_route, order.hold(cotangent)),
        smem=1,
    )
    order.note(cot)
    a0 = take(first_set, first_moving)
    a1 = net.by_core(a0)
    f0, f1 = (Columns(a, 0, cut) for a in (a0, a1))
    o0, o1 = (Columns(a, cut, a0.shape[1]) for a in (a0, a1))
    second_moving = first_moved(after(second_set, a0))
    second_set, second_moving = rest_moved(second_set, second_moving)
    third_set = order.note(stack_both([order.hold(third_parts[0])] + third_parts[1:], "weave"))
    third_moving = first_moved(third_set)
    near_tokens = after(tokens, third_set)
    above = lax.ppermute(near_tokens[rows - RADIUS :], AXES, step)
    below = lax.ppermute(near_tokens[:RADIUS], AXES, back)
    s0 = take(second_set, second_moving)
    s1 = net.by_core(s0)
    for j in range(1, net.levels):
        third_set = order.note(stack_both([third_set, order.hold(third_moving)]))
        third_moving = net.by_bit(third_set, j)
    (raw,) = run(
        prepare_body,
        "prepare",
        [((rows + 2 * RADIUS, width), BF16)],
        (order.hold(to_own), above, tokens, below),
    )
    order.note(raw)

    normed_ext, query_rows, pair_rows, vectors = run(
        light_rows_body,
        "light_rows",
        [
            ((rows + 2 * RADIUS, width), BF16),
            ((rows, light), BF16),
            ((rows + 2 * RADIUS, 2 * light), BF16),
            ((8, width), F32),
        ],
        (order.hold(raw), f0, f1),
    )
    order.note(query_rows)
    light_mixed, light_sums = run(
        light_forward_body,
        "light_forward",
        [((rows, light), BF16), ((rows, 128), F32)],
        (place, order.hold(query_rows), pair_rows),
        smem=1,
    )
    order.note(light_mixed)
    if packed:
        (keyed,) = run(
            functools.partial(heavy_rows_body, slots),
            "heavy_rows",
            [((keys, width), BF16)],
            (order.hold(vectors), to_own, s0, s1),
            scratch=[pltpu.VMEM((keys, width), BF16)],
        )
        order.note(keyed)
        heavy_pairs, routed, routed_query = run(
            heavy_pairs_body,
            "heavy_pairs",
            [((keys, 2 * heavy), BF16), ((slots, width), BF16), ((slots, heavy), BF16)],
            (order.hold(query_select), normed_ext, keyed, s0, s1),
        )
        order.note(routed_query)
        heavy_mixed, heavy_sums = run(
            heavy_forward_body,
            "heavy_forward",
            [((slots, heavy), BF16), ((2 * slots, 128), F32)],
            (query_docs, key_docs, order.hold(routed_query), heavy_pairs),
        )
    else:
        relative = net.target(jnp.arange(blocks, dtype=jnp.int32))
        near_routes = jnp.take(key_route, relative, axis=0)
        key_docs = document_of(relative[:, None] * rows + near_routes, lengths)
        key_docs = jnp.where(near_routes < rows, key_docs, -1).reshape(1, -1)
        keyed_raw = net.gather(nn(key_select, tokens).astype(BF16))
        keyed, heavy_pairs, routed, routed_query, heavy_mixed, heavy_sums = heavy_forward_wide(
            query_docs, key_docs, query_select, normed_ext, vectors, to_own,
            s0, s1, jnp.concatenate(keyed_raw, axis=0),
        )
    order.note(heavy_mixed)

    middle, normed_two, heavy_branch, feed_rows, feed_grads, sent = run(
        join_body,
        "join",
        [
            ((rows, width), F32),
            ((rows, width), BF16),
            ((slots, width), F32),
            ((slots, width), BF16),
            ((slots, width), F32),
            ((slots, 2 * width), BF16),
        ],
        (
            raw, light_mixed, order.hold(heavy_mixed), routed, query_select, feed_select, vectors, cot, to_own, o0, o1,
        ),
    )
    order.note(sent)

    got_parts = net.from_z(sent)
    got0 = take_z(got_parts)
    got1 = net.by_core(got0)
    t0, expert = part_both([third_set, order.hold(third_moving)], "part_both")
    order.note(t0)
    t1 = net.by_core(t0)
    keep, send, expert_keep, expert_send = run(
        expert_body,
        "expert",
        [
            ((pooled // 2, 2 * width), BF16),
            ((pooled // 2, 2 * width), BF16),
            ((half // 2, 6 * share), BF16),
            ((half // 2, 6 * share), BF16),
        ],
        (order.hold(got0), got1, to_slice, expert),
        scratch=[
            pltpu.VMEM((pooled, width), BF16),
            pltpu.VMEM((pooled, width), BF16),
            pltpu.VMEM((pooled, 2 * share), F32),
            pltpu.VMEM((pooled, share), F32),
            pltpu.VMEM((pooled, share), BF16),
            pltpu.VMEM((pooled, 2 * share), BF16),
        ],
    )
    order.note(send)
    moving = net.by_core(send)
    expert_moving = net.by_bit(expert_send, top_bit)
    feed_light, grad_normed, hidden, hidden_grads = run(
        feed_body,
        "feed",
        [
            ((rows, width), F32),
            ((rows, width), F32),
            ((rows, narrow), BF16),
            ((rows, 2 * narrow), BF16),
        ],
        (order.hold(normed_two), cot, t0, t1),
        scratch=[pltpu.VMEM((rows, 2 * narrow), F32), pltpu.VMEM((rows, narrow), F32)],
    )
    order.note(hidden)
    def give(keep, moved, pieces):
        out = fold(keep, order.hold(moved), pieces)
        order.note(out[0])
        return out

    def descend(keep, moved):
        for j in reversed(range(net.levels - 1)):
            keep, send = give(keep, moved, 2)
            moved = net.by_bit(send, j)
        return keep, moved

    summed = net.exchange_z(give(keep, moving, net.depth))
    third_keep, third_send = run(
        feed_weight_body,
        "feed_weight",
        [((half, 3 * narrow), BF16), ((half, 3 * narrow), BF16)],
        (order.hold(normed_two), cot, hidden, hidden_grads),
    )
    order.note(third_send)
    third_moving = net.by_core(third_send)

    third_keep, third_send = give(third_keep, third_moving, 2)
    third_moving = net.by_bit(third_send, top_bit)

    result, grad_middle, feed_vectors = run(
        turn_body,
        "turn",
        [((rows, width), BF16), ((rows, width), F32), ((8, width), F32)],
        (
            order.hold(summed[0]), *summed[1:], middle, feed_light, grad_normed, feed_rows, feed_grads, feed_select,
            vectors, cot, to_own,
        ),
    )
    order.note(grad_middle)
    if packed:
        grad_branch, grad_queries, grad_heavy_pairs, logits = run(
            heavy_scores_body,
            "heavy_scores",
            [
                ((slots, width), BF16),
                ((slots, heavy), BF16),
                ((keys, 2 * heavy), BF16),
                ((slots, 128), F32),
            ],
            (
                query_docs, key_docs, order.hold(grad_middle), query_select, routed, heavy_pairs, routed_query,
                heavy_branch, heavy_sums, vectors, o0, o1,
            ),
            scratch=[pltpu.VMEM((slots, heavy), BF16)],
        )
        order.note(grad_branch)
    expert_keep, expert_moving = descend(expert_keep, expert_moving)
    if packed:
        second_keep, second_send, heavy_vectors = run(
            heavy_weights_body,
            "heavy_weights",
            [
                ((half, 5 * width + light + width * rest // part), BF16),
                ((half, 5 * width + light + width * rest // part), BF16),
                ((8, width), F32),
            ],
            (
                grad_middle, routed, keyed, light_mixed, heavy_mixed, order.hold(grad_branch), grad_queries,
                grad_heavy_pairs, logits, vectors, to_own, s0, s1,
            ),
            scratch=[pltpu.VMEM((keys, width), BF16)],
        )
    else:
        second_keep, second_send, grad_routed, heavy_vectors, keyed_grads = heavy_backward_wide(
            grad_middle, query_select, routed, keyed, heavy_pairs, routed_query, light_mixed, heavy_mixed,
            heavy_branch, heavy_sums, vectors, to_own, o0.array[:, cut:], o1.array[:, cut:], s0, s1,
        )
    order.note(second_send)
    second_moving = net.by_core(second_send)
    third_keep, third_moving = descend(third_keep, third_moving)
    expert_parts = net.exchange_z(give(expert_keep, expert_moving, net.depth))
    if packed:
        (grad_routed,) = run(
            routed_body,
            "routed",
            [((slots, width), F32)],
            (order.hold(grad_queries), logits, vectors, s0, s1),
        )
        order.note(grad_routed)
    second_keep, second_send = give(second_keep, second_moving, 2)
    second_moving = net.by_bit(second_send, top_bit)
    grad_queries, grad_pairs = run(
        light_scores_body,
        "light_scores",
        [((rows, light), BF16), ((rows + 2 * RADIUS, 2 * light), BF16)],
        (place, order.hold(grad_middle), query_rows, pair_rows, light_sums, o0, o1),
        smem=1,
        scratch=[pltpu.VMEM((rows + 2 * RADIUS, 2 * light), F32), pltpu.VMEM((rows, light), BF16)],
    )
    order.note(grad_queries)
    third_parts = net.exchange_z(give(third_keep, third_moving, net.depth))
    first_keep, first_send, outer, grad_mine = run(
        light_weights_body,
        "light_weights",
        [
            ((half, 3 * light + 128), BF16),
            ((half, 3 * light + 128), BF16),
            ((2 * RADIUS, width), BF16),
            ((rows, width), F32),
        ],
        (
            raw, normed_ext, order.hold(grad_queries), grad_pairs, grad_routed, query_select, feed_vectors, heavy_vectors,
            to_own, f0, f1,
        ),
    )
    order.note(first_send)
    first_moving = net.by_core(first_send)
    from_next = lax.ppermute(outer[:RADIUS], AXES, back)
    from_prev = lax.ppermute(outer[RADIUS:], AXES, step)

    expert_keep, expert_send = take_apart([order.hold(expert_parts[0])] + expert_parts[1:], part)
    order.note(expert_send)
    expert_got = net.by_core(expert_send)
    third_grad = settle([order.hold(third_parts[0])] + third_parts[1:], [narrow] * 3, "settle_third")
    order.note(third_grad[0])
    second_keep, second_moving = descend(second_keep, second_moving)
    first_keep, first_send = give(first_keep, first_moving, 2)
    first_moving = net.by_bit(first_send, top_bit)
    (grad_near,) = run(
        halo_body, "halo", [((rows, width), F32)], (from_prev, from_next, order.hold(grad_mine), to_own)
    )
    order.note(grad_near)
    if packed:
        gate_grad, up_grad, down_grad = run(
            unpack_body,
            "unpack",
            [((part, wide), F32)] * 3,
            (place, order.hold(expert_keep), expert_got),
            smem=1,
        )
    else:
        expert_grad = jnp.concatenate([order.hold(expert_keep), expert_got], axis=0)
        expert_grad = jnp.take(expert_grad.reshape(members, part, 3 * share), net.members(), axis=0)
        expert_grad = expert_grad.reshape(members, part, 3, share).transpose(2, 1, 0, 3)
        gate_grad, up_grad, down_grad = expert_grad.reshape(3, part, wide).astype(F32)
    order.note(gate_grad)
    second_parts = net.exchange_z(give(second_keep, second_moving, net.depth))
    first_keep, first_moving = descend(first_keep, first_moving)
    first_parts = net.exchange_z(give(first_keep, first_moving, net.depth))
    widths = [width, light, heavy, heavy, heavy]
    if packed:
        widths.append(width + width * rest // part)
    second_grad = settle([order.hold(second_parts[0])] + second_parts[1:], widths, "settle_second")
    order.note(second_grad[0])
    if packed:
        keyed_own = second_grad[5]
    else:
        cut = keys // 2
        keyed_own = settle(net.reduce(keyed_grads[:cut], keyed_grads[cut:]), [width], "settle_keyed")[0]
    (tokens_grad,) = run(
        finish_body,
        "finish",
        [((rows, width), F32)],
        (order.hold(keyed_own), key_select, grad_near, grad_middle, raw, vectors, to_own),
    )
    order.note(tokens_grad)
    first_grad = settle(
        [order.hold(first_parts[0])] + first_parts[1:], [light, light, light, 128], "settle_first"
    )
    vector_out = first_grad[3][:, :4].T
    return (
        result,
        tokens_grad,
        first_grad[0],
        first_grad[1],
        first_grad[2],
        second_grad[1].T,
        second_grad[2],
        second_grad[3],
        second_grad[4],
        second_grad[0].T,
        vector_out[0],
        vector_out[1],
        third_grad[0],
        third_grad[1],
        third_grad[2].T,
        gate_grad,
        up_grad,
        down_grad.T,
        vector_out[2],
        vector_out[3],
    )


def solution(mesh):
    by_rows = P(AXES, None)
    by_columns = P(None, AXES)
    vector = P(AXES)
    return jax.shard_map(
        per_device,
        mesh=mesh,
        in_specs=(
            by_rows,
            by_rows,
            by_rows,
            by_rows,
            by_columns,
            by_rows,
            by_rows,
            by_rows,
            by_columns,
            vector,
            vector,
            by_rows,
            by_rows,
            by_columns,
            by_rows,
            by_rows,
            by_columns,
            vector,
            vector,
            P(),
            P(),
            P(),
            by_rows,
            by_rows,
        ),
        out_specs=(
            by_rows,
            by_rows,
            by_rows,
            by_rows,
            by_rows,
            by_columns,
            by_rows,
            by_rows,
            by_rows,
            by_columns,
            vector,
            vector,
            by_rows,
            by_rows,
            by_columns,
            by_rows,
            by_rows,
            by_columns,
            vector,
            vector,
        ),
        check_vma=False,
    )
```

profile of v0, /device:TPU:0, one launch (start us, length us, event | category | flops | bytes accessed | tf_op | source)
XLA Modules:
  0.0 265.2 jit_solution(5840310574186552579)
XLA Ops:
  3.6 5.0 %collective-permute-start.2 = (bf16[24,2944]{1,0:T(8,128)(2,1)}, bf16[24,2944]{1,0:T(8,128)(2,1)S(1)}, u32[]{:S(2)}, u32[]{:S(2)}) collective-permute-start(bf16[24,2944]{1,0:T(8,128)(2,1)} %pack_first.1.refs_0_), channel_id=1, source_target_pairs={{0,3},{1,2},{2,1},{3,0},{4,7},{5,6},{6,5},{7,4},{8,11},{9,10},{10,... | collective-permute-start | bytes 423944 | tf_op jit(solution)/shard_map/ppermute | solution.py:100
  13.6 7.2 %collective-permute-done.1.refs_2_ = bf16[24,2944]{1,0:T(8,128)(2,1)S(1)} collective-permute-done((bf16[24,2944]{1,0:T(8,128)(2,1)}, bf16[24,2944]{1,0:T(8,128)(2,1)S(1)}, u32[]{:S(2)}, u32[]{:S(2)}) %collective-permute-start.1) | collective-permute-done | bytes 141344 | tf_op jit(solution)/shard_map/ppermute | solution.py:100
  33.5 6.2 %collective-permute-done.6.refs_2_ = bf16[24,3328]{1,0:T(8,128)(2,1)S(1)} collective-permute-done((bf16[24,3328]{1,0:T(8,128)(2,1)}, bf16[24,3328]{1,0:T(8,128)(2,1)S(1)}, u32[]{:S(2)}, u32[]{:S(2)}) %collective-permute-start.6) | collective-permute-done | bytes 159776 | tf_op jit(solution)/shard_map/ppermute | solution.py:100
  41.0 6.8 %collective-permute-done.8.refs_1_ = bf16[192,2944]{1,0:T(8,128)(2,1)S(1)} collective-permute-done((bf16[192,2944]{1,0:T(8,128)(2,1)S(1)}, bf16[192,2944]{1,0:T(8,128)(2,1)S(1)}, u32[]{:S(2)}, u32[]{:S(2)}) %collective-permute-start.8) | collective-permute-done | bytes 1130528 | tf_op jit(solution)/shard_map/ppermute | solution.py:95
  49.8 3.1 %collective-permute-start.11 = (bf16[48,3072]{1,0:T(8,128)(2,1)S(1)}, bf16[48,3072]{1,0:T(8,128)(2,1)S(1)}, u32[]{:S(2)}, u32[]{:S(2)}) collective-permute-start(bf16[48,3072]{1,0:T(8,128)(2,1)S(1)} %get-tuple-element.210), channel_id=1, source_target_pairs={{0,2},{1,3},{2,0},{3,1},{4,6},{5,7},{6,4},{7,5},{8,10},{9,11},{10,... | collective-permute-start | bytes 884744 | tf_op jit(solution)/shard_map/ppermute | solution.py:100
  54.2 4.8 %collective-permute-done.9.refs_1_ = bf16[96,3328]{1,0:T(8,128)(2,1)S(1)} collective-permute-done((bf16[96,3328]{1,0:T(8,128)(2,1)S(1)}, bf16[96,3328]{1,0:T(8,128)(2,1)S(1)}, u32[]{:S(2)}, u32[]{:S(2)}) %collective-permute-start.9) | collective-permute-done | bytes 639008 | tf_op jit(solution)/shard_map/ppermute | solution.py:95
  61.6 11.4 %collective-permute-done.11.refs_2_ = bf16[48,3072]{1,0:T(8,128)(2,1)S(1)} collective-permute-done((bf16[48,3072]{1,0:T(8,128)(2,1)S(1)}, bf16[48,3072]{1,0:T(8,128)(2,1)S(1)}, u32[]{:S(2)}, u32[]{:S(2)}) %collective-permute-start.11) | collective-permute-done | bytes 294944 | tf_op jit(solution)/shard_map/ppermute | solution.py:100
  75.5 6.6 %collective-permute-start.15 = (bf16[128,768]{1,0:T(8,128)(2,1)S(1)}, bf16[128,768]{1,0:T(8,128)(2,1)S(1)}, u32[]{:S(2)}, u32[]{:S(2)}) collective-permute-start(bf16[128,768]{1,0:T(8,128)(2,1)S(1)} %get-tuple-element.363), channel_id=1, source_target_pairs={{0,1},{1,2},{2,3},{3,4},{4,5},{5,6},{6,7},{7,8},{8,9},{9,10},{10,1... | collective-permute-start | bytes 589832 | tf_op jit(solution)/shard_map/ppermute | solution.py:1150
  82.2 4.2 %collective-permute-done.14.refs_1_ = bf16[192,3328]{1,0:T(8,128)(2,1)S(1)} collective-permute-done((bf16[192,3328]{1,0:T(8,128)(2,1)S(1)}, bf16[192,3328]{1,0:T(8,128)(2,1)S(1)}, u32[]{:S(2)}, u32[]{:S(2)}) %collective-permute-start.14) | collective-permute-done | bytes 1277984 | tf_op jit(solution)/shard_map/ppermute | solution.py:95
  86.6 3.4 %collective-permute-done.13.refs_1_ = bf16[192,3072]{1,0:T(8,128)(2,1)S(1)} collective-permute-done((bf16[192,3072]{1,0:T(8,128)(2,1)S(1)}, bf16[192,3072]{1,0:T(8,128)(2,1)S(1)}, u32[]{:S(2)}, u32[]{:S(2)}) %collective-permute-start.13) | collective-permute-done | bytes 1179680 | tf_op jit(solution)/shard_map/ppermute | solution.py:95
  94.9 5.7 %light_forward.1 = (bf16[256,512]{1,0:T(8,128)(2,1)S(1)}, f32[256,128]{1,0:T(8,128)S(1)}) custom-call(s32[7]{0:T(128)S(1)} %copy-done.40, bf16[256,512]{1,0:T(8,128)(2,1)S(1)} %get-tuple-element.219.refs_1_.refs_2_, bf16[512,1024]{1,0:T(8,128)(2,1)S(1)} %get-tuple-element.220.refs_2_.refs_3_), custom_call_target="tpu_custom_call" | custom-call | flops 60000002048 | bytes 10000000000 | tf_op jit(solution)/shard_map/light_forward/pallas_call | solution.py:273
  103.4 4.4 %heavy_pairs.1 = (bf16[1024,1536]{1,0:T(8,128)(2,1)S(1)}, bf16[32,768]{1,0:T(8,128)(2,1)S(1)}, bf16[32,768]{1,0:T(8,128)(2,1)S(1)}) custom-call(bf16[32,256]{1,0:T(8,128)(2,1)S(1)} %get-tuple-element.227.refs_0_.refs_4_.refs_3_.refs_5_, bf16[512,768]{1,0:T(8,128)(2,1)S(1)} %get-tuple-element.228.refs_1_, bf16[1024,768]{1,0:T(8,128)(2,1)S(1)} %heavy_rows.1.refs_2_, ...), custom_call_target="tpu_custom_call" | custom-call | flops 60000002048 | bytes 10000000000 | tf_op jit(solution)/shard_map/heavy_pairs/pallas_call | solution.py:273
  107.9 3.4 %heavy_forward.1 = (bf16[32,768]{1,0:T(8,128)(2,1)S(1)}, f32[64,128]{1,0:T(8,128)S(1)}) custom-call(s32[32,1]{1,0:T(8,128)S(1)} %get-tuple-element.222.refs_0_, s32[1,1024]{1,0:T(1,128)S(1)} %copy-done.38, bf16[32,768]{1,0:T(8,128)(2,1)S(1)} %get-tuple-element.230.refs_2_.refs_6_, bf16[1024,1536]{1,0:T(8,128)(2,1)S(1)} %get-tuple-element.231.refs_3_.refs_5_), custom_call_target="tpu_custom_call" | custom-call | flops 50000000 | bytes 10000000000 | tf_op jit(solution)/shard_map/heavy_forward/pallas_call | solution.py:273
  115.2 3.5 %collective-permute-start.21 = (bf16[32,1536]{1,0:T(8,128)(2,1)S(1)}, bf16[32,1536]{1,0:T(8,128)(2,1)S(1)}, u32[]{:S(2)}, u32[]{:S(2)}) collective-permute-start(bf16[32,1536]{1,0:T(8,128)(2,1)S(1)} %get-tuple-element.237.refs_0_), channel_id=1, source_target_pairs={{0,3},{1,2},{2,1},{3,0},{4,7},{5,6},{6,5},{7,4},{8,11},{9,10},{10,... | collective-permute-start | bytes 294920 | tf_op jit(solution)/shard_map/ppermute | solution.py:100
  121.9 6.2 %collective-permute-done.20.refs_2_ = bf16[32,1536]{1,0:T(8,128)(2,1)S(1)} collective-permute-done((bf16[32,1536]{1,0:T(8,128)(2,1)S(1)}, bf16[32,1536]{1,0:T(8,128)(2,1)S(1)}, u32[]{:S(2)}, u32[]{:S(2)}) %collective-permute-start.20) | collective-permute-done | bytes 98336 | tf_op jit(solution)/shard_map/ppermute | solution.py:100
  129.9 5.9 %expert.1 = (bf16[128,1536]{1,0:T(8,128)(2,1)S(1)}, bf16[128,1536]{1,0:T(8,128)(2,1)S(1)}, bf16[192,3072]{1,0:T(8,128)(2,1)S(1)}, bf16[192,3072]{1,0:T(8,128)(2,1)S(1)}) custom-call(bf16[128,1536]{1,0:T(8,128)(2,1)S(1)} %stack.65.refs_0_, bf16[128,1536]{1,0:T(8,128)(2,1)S(1)} %collective-permute-done.23.refs_1_, ...), custom_call_target="tpu_custom_call" | custom-call | flops 60000002048 | bytes 10000000000 | tf_op jit(solution)/shard_map/expert/pallas_call | solution.py:273
  136.0 4.4 %feed.1 = (f32[256,768]{1,0:T(8,128)S(1)}, f32[256,768]{1,0:T(8,128)S(1)}, bf16[256,1024]{1,0:T(8,128)(2,1)S(1)}, bf16[256,2048]{1,0:T(8,128)(2,1)S(1)}) custom-call(bf16[256,768]{1,0:T(8,128)(2,1)S(1)} %get-tuple-element.250.refs_0_, bf16[256,768]{1,0:T(8,128)(2,1)S(1)} %get-tuple-element.202.refs_7_.refs_1_.refs_11_, ...), custom_call_target="tpu_custom_call" | custom-call | flops 60000002048 | bytes 10000000000 | tf_op jit(solution)/shard_map/feed/pallas_call | solution.py:273
  150.0 4.7 %collective-permute-done.28.refs_2_ = bf16[32,1536]{1,0:T(8,128)(2,1)S(1)} collective-permute-done((bf16[32,1536]{1,0:T(8,128)(2,1)S(1)}, bf16[32,1536]{1,0:T(8,128)(2,1)S(1)}, u32[]{:S(2)}, u32[]{:S(2)}) %collective-permute-start.28) | collective-permute-done | bytes 98336 | tf_op jit(solution)/shard_map/ppermute | solution.py:100
  154.8 2.8 %turn.1 = (bf16[256,768]{1,0:T(8,128)(2,1)}, f32[256,768]{1,0:T(8,128)S(1)}, f32[8,768]{1,0:T(8,128)S(1)}) custom-call(bf16[32,1536]{1,0:T(8,128)(2,1)S(1)} %get-tuple-element.256.refs_0_, bf16[32,1536]{1,0:T(8,128)(2,1)S(1)} %collective-permute-done.27.refs_1_, bf16[32,1536]{1,0:T(8,128)(2,1)S(1)} %collective-permute-done.28.refs_2_, ...), custom_call_target="tpu_custom_call" | custom-call | flops 5600000000 | bytes 10000000000 | tf_op jit(solution)/shard_map/turn/pallas_call | solution.py:273
  157.7 5.1 %heavy_scores.1 = (bf16[32,768]{1,0:T(8,128)(2,1)S(1)}, bf16[32,768]{1,0:T(8,128)(2,1)S(1)}, bf16[1024,1536]{1,0:T(8,128)(2,1)S(1)}, f32[32,128]{1,0:T(8,128)S(1)}) custom-call(s32[32,1]{1,0:T(8,128)S(1)} %copy-done.36, s32[1,1024]{1,0:T(1,128)S(1)} %copy-done.39, f32[256,768]{1,0:T(8,128)S(1)} %get-tuple-element.292.refs_2_.refs_0_.refs_1_.refs_3_, ...), custom_call_target="tpu_custom_call" | custom-call | flops 50000000 | bytes 10000000000 | tf_op jit(solution)/shard_map/heavy_scores/pallas_call | solution.py:273
  165.1 9.5 %heavy_weights.1 = (bf16[384,4608]{1,0:T(8,128)(2,1)S(1)}, bf16[384,4608]{1,0:T(8,128)(2,1)S(1)}, f32[8,768]{1,0:T(8,128)S(1)}) custom-call(f32[256,768]{1,0:T(8,128)S(1)} %get-tuple-element.292.refs_2_.refs_0_.refs_1_.refs_3_, bf16[32,768]{1,0:T(8,128)(2,1)S(1)} %copy-done.23, bf16[1024,768]{1,0:T(8,128)(2,1)S(1)} %copy-done.13, ...), custom_call_target="tpu_custom_call" | custom-call | flops 50000000 | bytes 10000000000 | tf_op jit(solution)/shard_map/heavy_weights/pallas_call | solution.py:273
  174.7 3.2 %collective-permute-done.33.refs_2_.refs_3_ = bf16[192,3072]{1,0:T(8,128)(2,1)S(1)} collective-permute-done((bf16[192,3072]{1,0:T(8,128)(2,1)S(1)}, bf16[192,3072]{1,0:T(8,128)(2,1)S(1)}, u32[]{:S(2)}, u32[]{:S(2)}) %collective-permute-start.33) | collective-permute-done | bytes 1179680 | tf_op jit(solution)/shard_map/ppermute | solution.py:95
  187.6 7.9 %light_scores.1 = (bf16[256,512]{1,0:T(8,128)(2,1)S(1)}, bf16[512,1024]{1,0:T(8,128)(2,1)S(1)}) custom-call(s32[7]{0:T(128)S(1)} %copy-done.41, f32[256,768]{1,0:T(8,128)S(1)} %get-tuple-element.292.refs_2_.refs_0_.refs_1_.refs_3_, bf16[256,512]{1,0:T(8,128)(2,1)S(1)} %copy-done.26, bf16[512,1024]{1,0:T(8,128)(2,1)S(1)} %copy-done.16, ...), custom_call_target="tpu_custom_call" | custom-call | flops 50000000 | bytes 10000000000 | tf_op jit(solution)/shard_map/light_scores/pallas_call | solution.py:273
  200.7 3.4 %light_weights.1 = (bf16[384,1664]{1,0:T(8,128)(2,1)S(1)}, bf16[384,1664]{1,0:T(8,128)(2,1)S(1)}, bf16[256,768]{1,0:T(8,128)(2,1)S(1)}, f32[256,768]{1,0:T(8,128)S(1)}) custom-call(bf16[512,768]{1,0:T(8,128)(2,1)S(1)} %copy-done.7, bf16[512,768]{1,0:T(8,128)(2,1)S(1)} %copy-done.20, bf16[256,512]{1,0:T(8,128)(2,1)S(1)} %get-tuple-element.297.refs_2_, ...), custom_call_target="tpu_custom_call" | custom-call | flops 50000000 | bytes 10000000000 | tf_op jit(solution)/shard_map/light_weights/pallas_call | solution.py:273
  204.3 7.2 %collective-permute-done.40.refs_2_ = bf16[24,3072]{1,0:T(8,128)(2,1)S(1)} collective-permute-done((bf16[24,3072]{1,0:T(8,128)(2,1)S(1)}, bf16[24,3072]{1,0:T(8,128)(2,1)S(1)}, u32[]{:S(2)}, u32[]{:S(2)}) %collective-permute-start.40) | collective-permute-done | bytes 147488 | tf_op jit(solution)/shard_map/ppermute | solution.py:100
  216.6 5.4 %collective-permute-start.43 = (bf16[128,768]{1,0:T(8,128)(2,1)S(1)}, bf16[128,768]{1,0:T(8,128)(2,1)S(1)}, u32[]{:S(2)}, u32[]{:S(2)}) collective-permute-start(bf16[128,768]{1,0:T(8,128)(2,1)S(1)} %get-tuple-element.361), channel_id=1, source_target_pairs={{0,1},{1,2},{2,3},{3,4},{4,5},{5,6},{6,7},{7,8},{8,9},{9,10},{10,1... | collective-permute-start | bytes 589832 | tf_op jit(solution)/shard_map/ppermute | solution.py:1390
  222.0 3.6 %collective-permute-done.44.refs_1_ = bf16[128,768]{1,0:T(8,128)(2,1)S(1)} collective-permute-done((bf16[128,768]{1,0:T(8,128)(2,1)S(1)}, bf16[128,768]{1,0:T(8,128)(2,1)S(1)}, u32[]{:S(2)}, u32[]{:S(2)}) %collective-permute-start.44) | collective-permute-done | bytes 196640 | tf_op jit(solution)/shard_map/ppermute | solution.py:1389
  229.0 2.9 %collective-permute-done.42.refs_4_.refs_5_.refs_6_.refs_7_ = bf16[96,4608]{1,0:T(8,128)(2,1)S(1)} collective-permute-done((bf16[96,4608]{1,0:T(8,128)(2,1)S(1)}, bf16[96,4608]{1,0:T(8,128)(2,1)S(1)}, u32[]{:S(2)}, u32[]{:S(2)}) %collective-permute-start.42) | collective-permute-done | bytes 884768 | tf_op jit(solution)/shard_map/ppermute | solution.py:95
  232.6 3.7 %collective-permute-start.48 = (bf16[96,1664]{1,0:T(8,128)(2,1)S(1)}, bf16[96,1664]{1,0:T(8,128)(2,1)S(1)}, u32[]{:S(2)}, u32[]{:S(2)}) collective-permute-start(bf16[96,1664]{1,0:T(8,128)(2,1)S(1)} %get-tuple-element.329), channel_id=1, source_target_pairs={{0,16},{1,17},{2,18},{3,19},{4,12},{5,13},{6,14},{7,15},{8,24},{9,... | collective-permute-start | bytes 958472 | tf_op jit(solution)/shard_map/ppermute | solution.py:95
  237.5 3.2 %collective-permute-start.51 = (bf16[24,4608]{1,0:T(8,128)(2,1)S(1)}, bf16[24,4608]{1,0:T(8,128)(2,1)S(1)}, u32[]{:S(2)}, u32[]{:S(2)}) collective-permute-start(bf16[24,4608]{1,0:T(8,128)(2,1)S(1)} %get-tuple-element.335), channel_id=1, source_target_pairs={{0,3},{1,2},{2,1},{3,0},{4,7},{5,6},{6,5},{7,4},{8,11},{9,10},{10,... | collective-permute-start | bytes 663560 | tf_op jit(solution)/shard_map/ppermute | solution.py:100
  243.8 4.0 %collective-permute-done.49.refs_1_ = bf16[24,4608]{1,0:T(8,128)(2,1)S(1)} collective-permute-done((bf16[24,4608]{1,0:T(8,128)(2,1)S(1)}, bf16[24,4608]{1,0:T(8,128)(2,1)S(1)}, u32[]{:S(2)}, u32[]{:S(2)}) %collective-permute-start.49) | collective-permute-done | bytes 221216 | tf_op jit(solution)/shard_map/ppermute | solution.py:100
  247.8 10.3 %collective-permute-done.50.refs_2_ = bf16[24,4608]{1,0:T(8,128)(2,1)S(1)} collective-permute-done((bf16[24,4608]{1,0:T(8,128)(2,1)S(1)}, bf16[24,4608]{1,0:T(8,128)(2,1)S(1)}, u32[]{:S(2)}, u32[]{:S(2)}) %collective-permute-start.50) | collective-permute-done | bytes 221216 | tf_op jit(solution)/shard_map/ppermute | solution.py:100
  (230 shorter events, 94.2 us)
Async XLA Ops:
  8.6 12.2 %collective-permute-start.1 = (bf16[24,2944]{1,0:T(8,128)(2,1)}, bf16[24,2944]{1,0:T(8,128)(2,1)S(1)}, u32[]{:S(2)}, u32[]{:S(2)}) collective-permute-start(bf16[24,2944]{1,0:T(8,128)(2,1)} %pack_first.1.refs_0_), channel_id=1, source_target_pairs={{0,2},{1,3},{2,0},{3,1},{4,6},{5,7},{6,4},{7,5},{8,10},{9,11},{10,... | collective-permute-start | bytes 423944 | tf_op jit(solution)/shard_map/ppermute | solution.py:100
  8.6 12.2 %collective-permute-start = (bf16[24,2944]{1,0:T(8,128)(2,1)}, bf16[24,2944]{1,0:T(8,128)(2,1)S(1)}, u32[]{:S(2)}, u32[]{:S(2)}) collective-permute-start(bf16[24,2944]{1,0:T(8,128)(2,1)} %pack_first.1.refs_0_), channel_id=1, source_target_pairs={{0,1},{1,0},{2,3},{3,2},{4,5},{5,4},{6,7},{7,6},{8,9},{9,8},{10,11... | collective-permute-start | bytes 423944 | tf_op jit(solution)/shard_map/ppermute | solution.py:100
  26.0 13.7 %collective-permute-start.6 = (bf16[24,3328]{1,0:T(8,128)(2,1)}, bf16[24,3328]{1,0:T(8,128)(2,1)S(1)}, u32[]{:S(2)}, u32[]{:S(2)}) collective-permute-start(bf16[24,3328]{1,0:T(8,128)(2,1)} %get-tuple-element.199.refs_0_), channel_id=1, source_target_pairs={{0,2},{1,3},{2,0},{3,1},{4,6},{5,7},{6,4},{7,5},{8,10},{9,11},{10,... | collective-permute-start | bytes 479240 | tf_op jit(solution)/shard_map/ppermute | solution.py:100
  26.0 13.7 %collective-permute-start.5 = (bf16[24,3328]{1,0:T(8,128)(2,1)}, bf16[24,3328]{1,0:T(8,128)(2,1)S(1)}, u32[]{:S(2)}, u32[]{:S(2)}) collective-permute-start(bf16[24,3328]{1,0:T(8,128)(2,1)} %get-tuple-element.199.refs_0_), channel_id=1, source_target_pairs={{0,1},{1,0},{2,3},{3,2},{4,5},{5,4},{6,7},{7,6},{8,9},{9,8},{10,11... | collective-permute-start | bytes 479240 | tf_op jit(solution)/shard_map/ppermute | solution.py:100
  32.0 15.7 %collective-permute-start.8 = (bf16[192,2944]{1,0:T(8,128)(2,1)S(1)}, bf16[192,2944]{1,0:T(8,128)(2,1)S(1)}, u32[]{:S(2)}, u32[]{:S(2)}) collective-permute-start(bf16[192,2944]{1,0:T(8,128)(2,1)S(1)} %stack.60.refs_0_), channel_id=1, source_target_pairs={{0,8},{1,9},{2,10},{3,11},{4,20},{5,21},{6,22},{7,23},{8,0},{9,1},... | collective-permute-start | bytes 3391496 | tf_op jit(solution)/shard_map/ppermute | solution.py:95
  49.8 11.8 %collective-permute-start.10 = (bf16[48,3072]{1,0:T(8,128)(2,1)S(1)}, bf16[48,3072]{1,0:T(8,128)(2,1)S(1)}, u32[]{:S(2)}, u32[]{:S(2)}) collective-permute-start(bf16[48,3072]{1,0:T(8,128)(2,1)S(1)} %get-tuple-element.208), channel_id=1, source_target_pairs={{0,1},{1,0},{2,3},{3,2},{4,5},{5,4},{6,7},{7,6},{8,9},{9,8},{10,11... | collective-permute-start | bytes 884744 | tf_op jit(solution)/shard_map/ppermute | solution.py:100
  49.8 23.2 %collective-permute-start.11 = (bf16[48,3072]{1,0:T(8,128)(2,1)S(1)}, bf16[48,3072]{1,0:T(8,128)(2,1)S(1)}, u32[]{:S(2)}, u32[]{:S(2)}) collective-permute-start(bf16[48,3072]{1,0:T(8,128)(2,1)S(1)} %get-tuple-element.210), channel_id=1, source_target_pairs={{0,2},{1,3},{2,0},{3,1},{4,6},{5,7},{6,4},{7,5},{8,10},{9,11},{10,... | collective-permute-start | bytes 884744 | tf_op jit(solution)/shard_map/ppermute | solution.py:100
  52.9 20.1 %collective-permute-start.12 = (bf16[48,3072]{1,0:T(8,128)(2,1)S(1)}, bf16[48,3072]{1,0:T(8,128)(2,1)S(1)}, u32[]{:S(2)}, u32[]{:S(2)}) collective-permute-start(bf16[48,3072]{1,0:T(8,128)(2,1)S(1)} %get-tuple-element.212), channel_id=1, source_target_pairs={{0,3},{1,2},{2,1},{3,0},{4,7},{5,6},{6,5},{7,4},{8,11},{9,10},{10,... | collective-permute-start | bytes 884744 | tf_op jit(solution)/shard_map/ppermute | solution.py:100
  54.2 38.8 %collective-permute-start.17 = (bf16[384,2944]{1,0:T(8,128)(2,1)S(1)}, bf16[384,2944]{1,0:T(8,128)(2,1)S(1)}, u32[]{:S(2)}, u32[]{:S(2)}) collective-permute-start(bf16[384,2944]{1,0:T(8,128)(2,1)S(1)} %stack.62.refs_1_.refs_9_.refs_10_.refs_5_), channel_id=1, source_target_pairs={{0,4},{1,5},{2,6},{3,7},{4,0},{5,1},{6,2},{7,3},{8,12},{9,13},{10,... | collective-permute-start | bytes 6782984 | tf_op jit(solution)/shard_map/ppermute | solution.py:91
  59.2 27.2 %collective-permute-start.14 = (bf16[192,3328]{1,0:T(8,128)(2,1)S(1)}, bf16[192,3328]{1,0:T(8,128)(2,1)S(1)}, u32[]{:S(2)}, u32[]{:S(2)}) collective-permute-start(bf16[192,3328]{1,0:T(8,128)(2,1)S(1)} %stack.63.refs_0_), channel_id=1, source_target_pairs={{0,8},{1,9},{2,10},{3,11},{4,20},{5,21},{6,22},{7,23},{8,0},{9,1},... | collective-permute-start | bytes 3833864 | tf_op jit(solution)/shard_map/ppermute | solution.py:95
  73.2 16.9 %collective-permute-start.13 = (bf16[192,3072]{1,0:T(8,128)(2,1)S(1)}, bf16[192,3072]{1,0:T(8,128)(2,1)S(1)}, u32[]{:S(2)}, u32[]{:S(2)}) collective-permute-start(bf16[192,3072]{1,0:T(8,128)(2,1)S(1)} %weave.1.refs_0_), channel_id=1, source_target_pairs={{0,16},{1,17},{2,18},{3,19},{4,12},{5,13},{6,14},{7,15},{8,24},{9,... | collective-permute-start | bytes 3538952 | tf_op jit(solution)/shard_map/ppermute | solution.py:95
  74.2 18.0 %collective-permute-start.16 = (bf16[128,768]{1,0:T(8,128)(2,1)S(1)}, bf16[128,768]{1,0:T(8,128)(2,1)S(1)}, u32[]{:S(2)}, u32[]{:S(2)}) collective-permute-start(bf16[128,768]{1,0:T(8,128)(2,1)S(1)} %get-tuple-element.362), channel_id=1, source_target_pairs={{1,0},{2,1},{3,2},{4,3},{5,4},{6,5},{7,6},{8,7},{9,8},{10,9},{11,1... | collective-permute-start | bytes 589832 | tf_op jit(solution)/shard_map/ppermute | solution.py:1151
  75.5 16.7 %collective-permute-start.15 = (bf16[128,768]{1,0:T(8,128)(2,1)S(1)}, bf16[128,768]{1,0:T(8,128)(2,1)S(1)}, u32[]{:S(2)}, u32[]{:S(2)}) collective-permute-start(bf16[128,768]{1,0:T(8,128)(2,1)S(1)} %get-tuple-element.363), channel_id=1, source_target_pairs={{0,1},{1,2},{2,3},{3,4},{4,5},{5,6},{6,7},{7,8},{8,9},{9,10},{10,1... | collective-permute-start | bytes 589832 | tf_op jit(solution)/shard_map/ppermute | solution.py:1150
  90.4 37.9 %collective-permute-start.22 = (bf16[384,3072]{1,0:T(8,128)(2,1)S(1)}, bf16[384,3072]{1,0:T(8,128)(2,1)S(1)}, u32[]{:S(2)}, u32[]{:S(2)}) collective-permute-start(bf16[384,3072]{1,0:T(8,128)(2,1)S(1)} %stack_both.1.refs_0_), channel_id=1, source_target_pairs={{0,8},{1,9},{2,10},{3,11},{4,20},{5,21},{6,22},{7,23},{8,0},{9,1},... | collective-permute-start | bytes 7077896 | tf_op jit(solution)/shard_map/ppermute | solution.py:95
  142.6 20.3 %collective-permute-start.30 = (bf16[192,3072]{1,0:T(8,128)(2,1)S(1)}, bf16[192,3072]{1,0:T(8,128)(2,1)S(1)}, u32[]{:S(2)}, u32[]{:S(2)}) collective-permute-start(bf16[192,3072]{1,0:T(8,128)(2,1)S(1)} %get-tuple-element.272), channel_id=1, source_target_pairs={{0,8},{1,9},{2,10},{3,11},{4,20},{5,21},{6,22},{7,23},{8,0},{9,1},... | collective-permute-start | bytes 3538952 | tf_op jit(solution)/shard_map/ppermute | solution.py:95
  149.9 28.0 %collective-permute-start.33 = (bf16[192,3072]{1,0:T(8,128)(2,1)S(1)}, bf16[192,3072]{1,0:T(8,128)(2,1)S(1)}, u32[]{:S(2)}, u32[]{:S(2)}) collective-permute-start(bf16[192,3072]{1,0:T(8,128)(2,1)S(1)} %get-tuple-element.282), channel_id=1, source_target_pairs={{0,8},{1,9},{2,10},{3,11},{4,20},{5,21},{6,22},{7,23},{8,0},{9,1},... | collective-permute-start | bytes 3538952 | tf_op jit(solution)/shard_map/ppermute | solution.py:95
  163.4 15.0 %collective-permute-start.32 = (bf16[96,3072]{1,0:T(8,128)(2,1)S(1)}, bf16[96,3072]{1,0:T(8,128)(2,1)S(1)}, u32[]{:S(2)}, u32[]{:S(2)}) collective-permute-start(bf16[96,3072]{1,0:T(8,128)(2,1)S(1)} %get-tuple-element.281), channel_id=1, source_target_pairs={{0,16},{1,17},{2,18},{3,19},{4,12},{5,13},{6,14},{7,15},{8,24},{9,... | collective-permute-start | bytes 1769480 | tf_op jit(solution)/shard_map/ppermute | solution.py:95
  178.6 16.9 %collective-permute-start.35 = (bf16[96,3072]{1,0:T(8,128)(2,1)S(1)}, bf16[96,3072]{1,0:T(8,128)(2,1)S(1)}, u32[]{:S(2)}, u32[]{:S(2)}) collective-permute-start(bf16[96,3072]{1,0:T(8,128)(2,1)S(1)} %get-tuple-element.291), channel_id=1, source_target_pairs={{0,16},{1,17},{2,18},{3,19},{4,12},{5,13},{6,14},{7,15},{8,24},{9,... | collective-permute-start | bytes 1769480 | tf_op jit(solution)/shard_map/ppermute | solution.py:95
  181.9 30.3 %collective-permute-start.34 = (bf16[192,4608]{1,0:T(8,128)(2,1)S(1)}, bf16[192,4608]{1,0:T(8,128)(2,1)S(1)}, u32[]{:S(2)}, u32[]{:S(2)}) collective-permute-start(bf16[192,4608]{1,0:T(8,128)(2,1)S(1)} %get-tuple-element.290), channel_id=1, source_target_pairs={{0,8},{1,9},{2,10},{3,11},{4,20},{5,21},{6,22},{7,23},{8,0},{9,1},... | collective-permute-start | bytes 5308424 | tf_op jit(solution)/shard_map/ppermute | solution.py:95
  183.1 13.8 %collective-permute-start.36 = (bf16[24,3072]{1,0:T(8,128)(2,1)S(1)}, bf16[24,3072]{1,0:T(8,128)(2,1)S(1)}, u32[]{:S(2)}, u32[]{:S(2)}) collective-permute-start(bf16[24,3072]{1,0:T(8,128)(2,1)S(1)} %get-tuple-element.303), channel_id=1, source_target_pairs={{0,1},{1,0},{2,3},{3,2},{4,5},{5,4},{6,7},{7,6},{8,9},{9,8},{10,11... | collective-permute-start | bytes 442376 | tf_op jit(solution)/shard_map/ppermute | solution.py:100
  185.2 13.7 %collective-permute-start.37 = (bf16[24,3072]{1,0:T(8,128)(2,1)S(1)}, bf16[24,3072]{1,0:T(8,128)(2,1)S(1)}, u32[]{:S(2)}, u32[]{:S(2)}) collective-permute-start(bf16[24,3072]{1,0:T(8,128)(2,1)S(1)} %get-tuple-element.304), channel_id=1, source_target_pairs={{0,2},{1,3},{2,0},{3,1},{4,6},{5,7},{6,4},{7,5},{8,10},{9,11},{10,... | collective-permute-start | bytes 442376 | tf_op jit(solution)/shard_map/ppermute | solution.py:100
  186.1 18.1 %collective-permute-start.38 = (bf16[24,3072]{1,0:T(8,128)(2,1)S(1)}, bf16[24,3072]{1,0:T(8,128)(2,1)S(1)}, u32[]{:S(2)}, u32[]{:S(2)}) collective-permute-start(bf16[24,3072]{1,0:T(8,128)(2,1)S(1)} %get-tuple-element.305), channel_id=1, source_target_pairs={{0,3},{1,2},{2,1},{3,0},{4,7},{5,6},{6,5},{7,4},{8,11},{9,10},{10,... | collective-permute-start | bytes 442376 | tf_op jit(solution)/shard_map/ppermute | solution.py:100
  197.0 14.5 %collective-permute-start.40 = (bf16[24,3072]{1,0:T(8,128)(2,1)S(1)}, bf16[24,3072]{1,0:T(8,128)(2,1)S(1)}, u32[]{:S(2)}, u32[]{:S(2)}) collective-permute-start(bf16[24,3072]{1,0:T(8,128)(2,1)S(1)} %get-tuple-element.309), channel_id=1, source_target_pairs={{0,2},{1,3},{2,0},{3,1},{4,6},{5,7},{6,4},{7,5},{8,10},{9,11},{10,... | collective-permute-start | bytes 442376 | tf_op jit(solution)/shard_map/ppermute | solution.py:100
  198.9 12.6 %collective-permute-start.41 = (bf16[24,3072]{1,0:T(8,128)(2,1)S(1)}, bf16[24,3072]{1,0:T(8,128)(2,1)S(1)}, u32[]{:S(2)}, u32[]{:S(2)}) collective-permute-start(bf16[24,3072]{1,0:T(8,128)(2,1)S(1)} %get-tuple-element.310), channel_id=1, source_target_pairs={{0,3},{1,2},{2,1},{3,0},{4,7},{5,6},{6,5},{7,4},{8,11},{9,10},{10,... | collective-permute-start | bytes 442376 | tf_op jit(solution)/shard_map/ppermute | solution.py:100
  212.8 19.1 %collective-permute-start.42 = (bf16[96,4608]{1,0:T(8,128)(2,1)S(1)}, bf16[96,4608]{1,0:T(8,128)(2,1)S(1)}, u32[]{:S(2)}, u32[]{:S(2)}) collective-permute-start(bf16[96,4608]{1,0:T(8,128)(2,1)S(1)} %get-tuple-element.314), channel_id=1, source_target_pairs={{0,16},{1,17},{2,18},{3,19},{4,12},{5,13},{6,14},{7,15},{8,24},{9,... | collective-permute-start | bytes 2654216 | tf_op jit(solution)/shard_map/ppermute | solution.py:95
  214.4 17.9 %collective-permute-start.47 = (bf16[192,1664]{1,0:T(8,128)(2,1)S(1)}, bf16[192,1664]{1,0:T(8,128)(2,1)S(1)}, u32[]{:S(2)}, u32[]{:S(2)}) collective-permute-start(bf16[192,1664]{1,0:T(8,128)(2,1)S(1)} %get-tuple-element.326), channel_id=1, source_target_pairs={{0,8},{1,9},{2,10},{3,11},{4,20},{5,21},{6,22},{7,23},{8,0},{9,1},... | collective-permute-start | bytes 1916936 | tf_op jit(solution)/shard_map/ppermute | solution.py:95
  215.3 12.1 %collective-permute-start.46 = (bf16[96,1536]{1,0:T(8,128)(2,1)S(1)}, bf16[96,1536]{1,0:T(8,128)(2,1)S(1)}, u32[]{:S(2)}, u32[]{:S(2)}) collective-permute-start(bf16[96,1536]{1,0:T(8,128)(2,1)S(1)} %get-tuple-element.306), channel_id=1, source_target_pairs={{0,4},{1,5},{2,6},{3,7},{4,0},{5,1},{6,2},{7,3},{8,12},{9,13},{10,... | collective-permute-start | bytes 884744 | tf_op jit(solution)/shard_map/ppermute | solution.py:91
  236.6 21.5 %collective-permute-start.50 = (bf16[24,4608]{1,0:T(8,128)(2,1)S(1)}, bf16[24,4608]{1,0:T(8,128)(2,1)S(1)}, u32[]{:S(2)}, u32[]{:S(2)}) collective-permute-start(bf16[24,4608]{1,0:T(8,128)(2,1)S(1)} %get-tuple-element.334), channel_id=1, source_target_pairs={{0,2},{1,3},{2,0},{3,1},{4,6},{5,7},{6,4},{7,5},{8,10},{9,11},{10,... | collective-permute-start | bytes 663560 | tf_op jit(solution)/shard_map/ppermute | solution.py:100
  237.5 20.7 %collective-permute-start.51 = (bf16[24,4608]{1,0:T(8,128)(2,1)S(1)}, bf16[24,4608]{1,0:T(8,128)(2,1)S(1)}, u32[]{:S(2)}, u32[]{:S(2)}) collective-permute-start(bf16[24,4608]{1,0:T(8,128)(2,1)S(1)} %get-tuple-element.335), channel_id=1, source_target_pairs={{0,3},{1,2},{2,1},{3,0},{4,7},{5,6},{6,5},{7,4},{8,11},{9,10},{10,... | collective-permute-start | bytes 663560 | tf_op jit(solution)/shard_map/ppermute | solution.py:100
  241.4 19.9 %collective-permute-start.52 = (bf16[24,1664]{1,0:T(8,128)(2,1)S(1)}, bf16[24,1664]{1,0:T(8,128)(2,1)S(1)}, u32[]{:S(2)}, u32[]{:S(2)}) collective-permute-start(bf16[24,1664]{1,0:T(8,128)(2,1)S(1)} %get-tuple-element.341), channel_id=1, source_target_pairs={{0,1},{1,0},{2,3},{3,2},{4,5},{5,4},{6,7},{7,6},{8,9},{9,8},{10,11... | collective-permute-start | bytes 239624 | tf_op jit(solution)/shard_map/ppermute | solution.py:100
  242.9 20.9 %collective-permute-start.53 = (bf16[24,1664]{1,0:T(8,128)(2,1)S(1)}, bf16[24,1664]{1,0:T(8,128)(2,1)S(1)}, u32[]{:S(2)}, u32[]{:S(2)}) collective-permute-start(bf16[24,1664]{1,0:T(8,128)(2,1)S(1)} %get-tuple-element.342), channel_id=1, source_target_pairs={{0,2},{1,3},{2,0},{3,1},{4,6},{5,7},{6,4},{7,5},{8,10},{9,11},{10,... | collective-permute-start | bytes 239624 | tf_op jit(solution)/shard_map/ppermute | solution.py:100
  247.8 16.0 %collective-permute-start.54 = (bf16[24,1664]{1,0:T(8,128)(2,1)S(1)}, bf16[24,1664]{1,0:T(8,128)(2,1)S(1)}, u32[]{:S(2)}, u32[]{:S(2)}) collective-permute-start(bf16[24,1664]{1,0:T(8,128)(2,1)S(1)} %get-tuple-element.343), channel_id=1, source_target_pairs={{0,3},{1,2},{2,1},{3,0},{4,7},{5,6},{6,5},{7,4},{8,11},{9,10},{10,... | collective-permute-start | bytes 239624 | tf_op jit(solution)/shard_map/ppermute | solution.py:100
  (68 other events, 702.4 us)
where the time goes:
time: 266 us; the launch traced here: 265 us
  waiting for transfers between devices  96.2 us (36%)
  Pallas kernels  82.1 us (31%)
  starting transfers between devices  75.9 us (29%)
  local copies, waits for them, and re-layouts  7.92 us (3%)
    pallas_call x38, Pallas kernels, run(): pl.pallas_call(kernel, name=name, compiler_params=pltpu.CompilerParams(vm...  76.7 us
    ppermute x27, waiting for transfers between devices, by_z(): return lax.ppermute(array, AXES, self.pairs(lambda p, c, z: (p, c, z ^ k)))  63.1 us
    ppermute x27, starting transfers between devices, by_z(): return lax.ppermute(array, AXES, self.pairs(lambda p, c, z: (p, c, z ^ k)))  39.2 us
    ppermute x14, waiting for transfers between devices, by_bit(): lax.ppermute(array, AXES, self.pairs(lambda p, c, z: (p ^ 1 << (j if c el...  27.2 us
    ppermute x14, starting transfers between devices, by_bit(): lax.ppermute(array, AXES, self.pairs(lambda p, c, z: (p ^ 1 << (j if c el...  18.8 us
    ppermute x1, starting transfers between devices, per_device(): above = lax.ppermute(near_tokens[rows - RADIUS:], AXES, step)  6.62 us
    ppermute x1, starting transfers between devices, per_device(): from_prev = lax.ppermute(outer[RADIUS:], AXES, step)  5.39 us
    pallas_call x12, Pallas kernels, fold(): pl.pallas_call(body, name='fold', compiler_params=pltpu.CompilerParams(vm...  5.37 us
  transfers between devices with their start and end apart: 55, of which 24 were waited for; matrix products, arithmetic and copies ran while one was open for 1% of the time, Pallas kernels for 29%

commit v1 on v0

--- a/solution.py
+++ b/solution.py
@@ -133,7 +133,7 @@
 
 
 def by_columns(width, step):
-    chunk = 256 if width % 256 == 0 else 128
+    chunk = next(c for c in (512, 256, 128, width) if width % c == 0)
     if width % chunk or width <= 4 * chunk:
         step(slice(0, width))
         return
@@ -1151,9 +1151,6 @@
     below = lax.ppermute(near_tokens[:RADIUS], AXES, back)
     s0 = take(second_set, second_moving)
     s1 = net.by_core(s0)
-    for j in range(1, net.levels):
-        third_set = order.note(stack_both([third_set, order.hold(third_moving)]))
-        third_moving = net.by_bit(third_set, j)
     (raw,) = run(
         prepare_body,
         "prepare",
@@ -1174,6 +1171,9 @@
         (order.hold(raw), f0, f1),
     )
     order.note(query_rows)
+    for j in range(1, net.levels):
+        third_set = order.note(stack_both([third_set, order.hold(third_moving)]))
+        third_moving = net.by_bit(third_set, j)
     light_mixed, light_sums = run(
         light_forward_body,
         "light_forward",

time: 266 us -> 261 us (0.981)
  no operation moved by 1% of the time
where the time goes in v1:
time: 261 us
  waiting for transfers between devices  93.9 us (36%)
  Pallas kernels  80.7 us (31%)
  starting transfers between devices  75.1 us (29%)
  local copies, waits for them, and re-layouts  8.14 us (3%)
    pallas_call x38, Pallas kernels, run(): pl.pallas_call(kernel, name=name, compiler_params=pltpu.CompilerParams(vm...  76.1 us
    ppermute x27, waiting for transfers between devices, by_z(): return lax.ppermute(array, AXES, self.pairs(lambda p, c, z: (p, c, z ^ k)))  62.7 us
    ppermute x27, starting transfers between devices, by_z(): return lax.ppermute(array, AXES, self.pairs(lambda p, c, z: (p, c, z ^ k)))  39 us
    ppermute x14, waiting for transfers between devices, by_bit(): lax.ppermute(array, AXES, self.pairs(lambda p, c, z: (p ^ 1 << (j if c el...  24.7 us
    ppermute x14, starting transfers between devices, by_bit(): lax.ppermute(array, AXES, self.pairs(lambda p, c, z: (p ^ 1 << (j if c el...  19.8 us
    ppermute x1, starting transfers between devices, per_device(): above = lax.ppermute(near_tokens[rows - RADIUS:], AXES, step)  6.62 us
    ppermute x1, starting transfers between devices, per_device(): from_prev = lax.ppermute(outer[RADIUS:], AXES, step)  5.61 us
    unnamed x90, local copies, waits for them, and re-layouts  5.4 us
  transfers between devices with their start and end apart: 55, of which 24 were waited for; matrix products, arithmetic and copies ran while one was open for 1% of the time, Pallas kernels for 29%

profile of v1, /device:TPU:0, one launch (start us, length us, event | category | flops | bytes accessed | tf_op | source)
XLA Modules:
  0.0 261.0 jit_solution(5861034051765805517)
XLA Ops:
  3.6 5.0 %collective-permute-start.2 = (bf16[24,2944]{1,0:T(8,128)(2,1)}, bf16[24,2944]{1,0:T(8,128)(2,1)S(1)}, u32[]{:S(2)}, u32[]{:S(2)}) collective-permute-start(bf16[24,2944]{1,0:T(8,128)(2,1)} %pack_first.1.refs_0_), channel_id=1, source_target_pairs={{0,3},{1,2},{2,1},{3,0},{4,7},{5,6},{6,5},{7,4},{8,11},{9,10},{10,... | collective-permute-start | bytes 423944 | tf_op jit(solution)/shard_map/ppermute | solution.py:100
  13.6 7.2 %collective-permute-done.1.refs_2_ = bf16[24,2944]{1,0:T(8,128)(2,1)S(1)} collective-permute-done((bf16[24,2944]{1,0:T(8,128)(2,1)}, bf16[24,2944]{1,0:T(8,128)(2,1)S(1)}, u32[]{:S(2)}, u32[]{:S(2)}) %collective-permute-start.1) | collective-permute-done | bytes 141344 | tf_op jit(solution)/shard_map/ppermute | solution.py:100
  33.5 6.2 %collective-permute-done.6.refs_2_ = bf16[24,3328]{1,0:T(8,128)(2,1)S(1)} collective-permute-done((bf16[24,3328]{1,0:T(8,128)(2,1)}, bf16[24,3328]{1,0:T(8,128)(2,1)S(1)}, u32[]{:S(2)}, u32[]{:S(2)}) %collective-permute-start.6) | collective-permute-done | bytes 159776 | tf_op jit(solution)/shard_map/ppermute | solution.py:100
  41.0 6.8 %collective-permute-done.8.refs_1_ = bf16[192,2944]{1,0:T(8,128)(2,1)S(1)} collective-permute-done((bf16[192,2944]{1,0:T(8,128)(2,1)S(1)}, bf16[192,2944]{1,0:T(8,128)(2,1)S(1)}, u32[]{:S(2)}, u32[]{:S(2)}) %collective-permute-start.8) | collective-permute-done | bytes 1130528 | tf_op jit(solution)/shard_map/ppermute | solution.py:95
  49.8 3.1 %collective-permute-start.12 = (bf16[48,3072]{1,0:T(8,128)(2,1)S(1)}, bf16[48,3072]{1,0:T(8,128)(2,1)S(1)}, u32[]{:S(2)}, u32[]{:S(2)}) collective-permute-start(bf16[48,3072]{1,0:T(8,128)(2,1)S(1)} %get-tuple-element.210), channel_id=1, source_target_pairs={{0,2},{1,3},{2,0},{3,1},{4,6},{5,7},{6,4},{7,5},{8,10},{9,11},{10,... | collective-permute-start | bytes 884744 | tf_op jit(solution)/shard_map/ppermute | solution.py:100
  54.2 4.8 %collective-permute-done.9.refs_1_ = bf16[96,3328]{1,0:T(8,128)(2,1)S(1)} collective-permute-done((bf16[96,3328]{1,0:T(8,128)(2,1)S(1)}, bf16[96,3328]{1,0:T(8,128)(2,1)S(1)}, u32[]{:S(2)}, u32[]{:S(2)}) %collective-permute-start.9) | collective-permute-done | bytes 639008 | tf_op jit(solution)/shard_map/ppermute | solution.py:95
  61.6 11.4 %collective-permute-done.12.refs_2_ = bf16[48,3072]{1,0:T(8,128)(2,1)S(1)} collective-permute-done((bf16[48,3072]{1,0:T(8,128)(2,1)S(1)}, bf16[48,3072]{1,0:T(8,128)(2,1)S(1)}, u32[]{:S(2)}, u32[]{:S(2)}) %collective-permute-start.12) | collective-permute-done | bytes 294944 | tf_op jit(solution)/shard_map/ppermute | solution.py:100
  75.5 6.6 %collective-permute-start.14 = (bf16[128,768]{1,0:T(8,128)(2,1)S(1)}, bf16[128,768]{1,0:T(8,128)(2,1)S(1)}, u32[]{:S(2)}, u32[]{:S(2)}) collective-permute-start(bf16[128,768]{1,0:T(8,128)(2,1)S(1)} %get-tuple-element.363), channel_id=1, source_target_pairs={{0,1},{1,2},{2,3},{3,4},{4,5},{5,6},{6,7},{7,8},{8,9},{9,10},{10,1... | collective-permute-start | bytes 589832 | tf_op jit(solution)/shard_map/ppermute | solution.py:1150
  82.1 4.4 %collective-permute-done.10.refs_1_ = bf16[192,3328]{1,0:T(8,128)(2,1)S(1)} collective-permute-done((bf16[192,3328]{1,0:T(8,128)(2,1)S(1)}, bf16[192,3328]{1,0:T(8,128)(2,1)S(1)}, u32[]{:S(2)}, u32[]{:S(2)}) %collective-permute-start.10) | collective-permute-done | bytes 1277984 | tf_op jit(solution)/shard_map/ppermute | solution.py:95
  92.2 5.7 %light_forward.1 = (bf16[256,512]{1,0:T(8,128)(2,1)S(1)}, f32[256,128]{1,0:T(8,128)S(1)}) custom-call(s32[7]{0:T(128)S(1)} %copy-done.40, bf16[256,512]{1,0:T(8,128)(2,1)S(1)} %get-tuple-element.219.refs_1_.refs_2_, bf16[512,1024]{1,0:T(8,128)(2,1)S(1)} %get-tuple-element.220.refs_2_.refs_3_), custom_call_target="tpu_custom_call" | custom-call | flops 60000002048 | bytes 10000000000 | tf_op jit(solution)/shard_map/light_forward/pallas_call | solution.py:273
  97.9 2.8 %heavy_rows.1.refs_2_ = bf16[1024,768]{1,0:T(8,128)(2,1)S(1)} custom-call(f32[8,768]{1,0:T(8,128)S(1)} %get-tuple-element.226.refs_0_.refs_6_.refs_10_.refs_9_.refs_2_.refs_5_, bf16[768,768]{1,0:T(8,128)(2,1)S(1)} %get-tuple-element.214.refs_1_.refs_0_.refs_8_.refs_12_.refs_10_.refs_3_.refs_6_, bf16[384,3328]{1,0:T(8,128)(2,1)S(1)} %stack.64.refs_2_.refs_3_.refs_11_, ...), custom_call_target="tpu_custom_call" | custom-call | flops 50000000 | bytes 10000000000 | tf_op jit(solution)/shard_map/heavy_rows/pallas_call | solution.py:273
  100.7 4.4 %heavy_pairs.1 = (bf16[1024,1536]{1,0:T(8,128)(2,1)S(1)}, bf16[32,768]{1,0:T(8,128)(2,1)S(1)}, bf16[32,768]{1,0:T(8,128)(2,1)S(1)}) custom-call(bf16[32,256]{1,0:T(8,128)(2,1)S(1)} %get-tuple-element.227.refs_0_.refs_4_.refs_3_.refs_5_, bf16[512,768]{1,0:T(8,128)(2,1)S(1)} %get-tuple-element.228.refs_1_, bf16[1024,768]{1,0:T(8,128)(2,1)S(1)} %heavy_rows.1.refs_2_, ...), custom_call_target="tpu_custom_call" | custom-call | flops 60000002048 | bytes 10000000000 | tf_op jit(solution)/shard_map/heavy_pairs/pallas_call | solution.py:273
  105.2 3.4 %heavy_forward.1 = (bf16[32,768]{1,0:T(8,128)(2,1)S(1)}, f32[64,128]{1,0:T(8,128)S(1)}) custom-call(s32[32,1]{1,0:T(8,128)S(1)} %get-tuple-element.222.refs_0_, s32[1,1024]{1,0:T(1,128)S(1)} %copy-done.38, bf16[32,768]{1,0:T(8,128)(2,1)S(1)} %get-tuple-element.230.refs_2_.refs_6_, bf16[1024,1536]{1,0:T(8,128)(2,1)S(1)} %get-tuple-element.231.refs_3_.refs_5_), custom_call_target="tpu_custom_call" | custom-call | flops 50000000 | bytes 10000000000 | tf_op jit(solution)/shard_map/heavy_forward/pallas_call | solution.py:273
  116.9 3.1 %collective-permute-done.21.refs_3_ = bf16[32,1536]{1,0:T(8,128)(2,1)S(1)} collective-permute-done((bf16[32,1536]{1,0:T(8,128)(2,1)S(1)}, bf16[32,1536]{1,0:T(8,128)(2,1)S(1)}, u32[]{:S(2)}, u32[]{:S(2)}) %collective-permute-start.21) | collective-permute-done | bytes 98336 | tf_op jit(solution)/shard_map/ppermute | solution.py:100
  120.1 4.7 %collective-permute-done.20.refs_2_ = bf16[32,1536]{1,0:T(8,128)(2,1)S(1)} collective-permute-done((bf16[32,1536]{1,0:T(8,128)(2,1)S(1)}, bf16[32,1536]{1,0:T(8,128)(2,1)S(1)}, u32[]{:S(2)}, u32[]{:S(2)}) %collective-permute-start.20) | collective-permute-done | bytes 98336 | tf_op jit(solution)/shard_map/ppermute | solution.py:100
  126.6 5.9 %expert.1 = (bf16[128,1536]{1,0:T(8,128)(2,1)S(1)}, bf16[128,1536]{1,0:T(8,128)(2,1)S(1)}, bf16[192,3072]{1,0:T(8,128)(2,1)S(1)}, bf16[192,3072]{1,0:T(8,128)(2,1)S(1)}) custom-call(bf16[128,1536]{1,0:T(8,128)(2,1)S(1)} %stack.65.refs_0_, bf16[128,1536]{1,0:T(8,128)(2,1)S(1)} %collective-permute-done.23.refs_1_, ...), custom_call_target="tpu_custom_call" | custom-call | flops 60000002048 | bytes 10000000000 | tf_op jit(solution)/shard_map/expert/pallas_call | solution.py:273
  132.7 4.4 %feed.1 = (f32[256,768]{1,0:T(8,128)S(1)}, f32[256,768]{1,0:T(8,128)S(1)}, bf16[256,1024]{1,0:T(8,128)(2,1)S(1)}, bf16[256,2048]{1,0:T(8,128)(2,1)S(1)}) custom-call(bf16[256,768]{1,0:T(8,128)(2,1)S(1)} %get-tuple-element.250.refs_0_, bf16[256,768]{1,0:T(8,128)(2,1)S(1)} %get-tuple-element.201.refs_7_.refs_1_.refs_11_, ...), custom_call_target="tpu_custom_call" | custom-call | flops 60000002048 | bytes 10000000000 | tf_op jit(solution)/shard_map/feed/pallas_call | solution.py:273
  146.3 4.9 %collective-permute-done.28.refs_2_ = bf16[32,1536]{1,0:T(8,128)(2,1)S(1)} collective-permute-done((bf16[32,1536]{1,0:T(8,128)(2,1)S(1)}, bf16[32,1536]{1,0:T(8,128)(2,1)S(1)}, u32[]{:S(2)}, u32[]{:S(2)}) %collective-permute-start.28) | collective-permute-done | bytes 98336 | tf_op jit(solution)/shard_map/ppermute | solution.py:100
  151.3 2.8 %turn.1 = (bf16[256,768]{1,0:T(8,128)(2,1)}, f32[256,768]{1,0:T(8,128)S(1)}, f32[8,768]{1,0:T(8,128)S(1)}) custom-call(bf16[32,1536]{1,0:T(8,128)(2,1)S(1)} %get-tuple-element.256.refs_0_, bf16[32,1536]{1,0:T(8,128)(2,1)S(1)} %collective-permute-done.27.refs_1_, bf16[32,1536]{1,0:T(8,128)(2,1)S(1)} %collective-permute-done.28.refs_2_, ...), custom_call_target="tpu_custom_call" | custom-call | flops 5600000000 | bytes 10000000000 | tf_op jit(solution)/shard_map/turn/pallas_call | solution.py:273
  154.2 5.1 %heavy_scores.1 = (bf16[32,768]{1,0:T(8,128)(2,1)S(1)}, bf16[32,768]{1,0:T(8,128)(2,1)S(1)}, bf16[1024,1536]{1,0:T(8,128)(2,1)S(1)}, f32[32,128]{1,0:T(8,128)S(1)}) custom-call(s32[32,1]{1,0:T(8,128)S(1)} %copy-done.36, s32[1,1024]{1,0:T(1,128)S(1)} %copy-done.39, f32[256,768]{1,0:T(8,128)S(1)} %get-tuple-element.292.refs_2_.refs_0_.refs_1_.refs_3_, ...), custom_call_target="tpu_custom_call" | custom-call | flops 50000000 | bytes 10000000000 | tf_op jit(solution)/shard_map/heavy_scores/pallas_call | solution.py:273
  161.5 9.5 %heavy_weights.1 = (bf16[384,4608]{1,0:T(8,128)(2,1)S(1)}, bf16[384,4608]{1,0:T(8,128)(2,1)S(1)}, f32[8,768]{1,0:T(8,128)S(1)}) custom-call(f32[256,768]{1,0:T(8,128)S(1)} %get-tuple-element.292.refs_2_.refs_0_.refs_1_.refs_3_, bf16[32,768]{1,0:T(8,128)(2,1)S(1)} %copy-done.23, bf16[1024,768]{1,0:T(8,128)(2,1)S(1)} %copy-done.13, ...), custom_call_target="tpu_custom_call" | custom-call | flops 50000000 | bytes 10000000000 | tf_op jit(solution)/shard_map/heavy_weights/pallas_call | solution.py:273
  171.1 3.3 %collective-permute-done.33.refs_2_.refs_3_ = bf16[192,3072]{1,0:T(8,128)(2,1)S(1)} collective-permute-done((bf16[192,3072]{1,0:T(8,128)(2,1)S(1)}, bf16[192,3072]{1,0:T(8,128)(2,1)S(1)}, u32[]{:S(2)}, u32[]{:S(2)}) %collective-permute-start.33) | collective-permute-done | bytes 1179680 | tf_op jit(solution)/shard_map/ppermute | solution.py:95
  184.0 7.9 %light_scores.1 = (bf16[256,512]{1,0:T(8,128)(2,1)S(1)}, bf16[512,1024]{1,0:T(8,128)(2,1)S(1)}) custom-call(s32[7]{0:T(128)S(1)} %copy-done.41, f32[256,768]{1,0:T(8,128)S(1)} %get-tuple-element.292.refs_2_.refs_0_.refs_1_.refs_3_, bf16[256,512]{1,0:T(8,128)(2,1)S(1)} %copy-done.26, bf16[512,1024]{1,0:T(8,128)(2,1)S(1)} %copy-done.16, ...), custom_call_target="tpu_custom_call" | custom-call | flops 50000000 | bytes 10000000000 | tf_op jit(solution)/shard_map/light_scores/pallas_call | solution.py:273
  197.0 3.4 %light_weights.1 = (bf16[384,1664]{1,0:T(8,128)(2,1)S(1)}, bf16[384,1664]{1,0:T(8,128)(2,1)S(1)}, bf16[256,768]{1,0:T(8,128)(2,1)S(1)}, f32[256,768]{1,0:T(8,128)S(1)}) custom-call(bf16[512,768]{1,0:T(8,128)(2,1)S(1)} %copy-done.7, bf16[512,768]{1,0:T(8,128)(2,1)S(1)} %copy-done.20, bf16[256,512]{1,0:T(8,128)(2,1)S(1)} %get-tuple-element.297.refs_2_, ...), custom_call_target="tpu_custom_call" | custom-call | flops 50000000 | bytes 10000000000 | tf_op jit(solution)/shard_map/light_weights/pallas_call | solution.py:273
  200.6 7.2 %collective-permute-done.40.refs_2_ = bf16[24,3072]{1,0:T(8,128)(2,1)S(1)} collective-permute-done((bf16[24,3072]{1,0:T(8,128)(2,1)S(1)}, bf16[24,3072]{1,0:T(8,128)(2,1)S(1)}, u32[]{:S(2)}, u32[]{:S(2)}) %collective-permute-start.40) | collective-permute-done | bytes 147488 | tf_op jit(solution)/shard_map/ppermute | solution.py:100
  212.8 5.6 %collective-permute-start.43 = (bf16[128,768]{1,0:T(8,128)(2,1)S(1)}, bf16[128,768]{1,0:T(8,128)(2,1)S(1)}, u32[]{:S(2)}, u32[]{:S(2)}) collective-permute-start(bf16[128,768]{1,0:T(8,128)(2,1)S(1)} %get-tuple-element.361), channel_id=1, source_target_pairs={{0,1},{1,2},{2,3},{3,4},{4,5},{5,6},{6,7},{7,8},{8,9},{9,10},{10,1... | collective-permute-start | bytes 589832 | tf_op jit(solution)/shard_map/ppermute | solution.py:1390
  218.4 3.6 %collective-permute-done.44.refs_1_ = bf16[128,768]{1,0:T(8,128)(2,1)S(1)} collective-permute-done((bf16[128,768]{1,0:T(8,128)(2,1)S(1)}, bf16[128,768]{1,0:T(8,128)(2,1)S(1)}, u32[]{:S(2)}, u32[]{:S(2)}) %collective-permute-start.44) | collective-permute-done | bytes 196640 | tf_op jit(solution)/shard_map/ppermute | solution.py:1389
  225.4 3.2 %collective-permute-done.42.refs_4_.refs_5_.refs_6_.refs_7_ = bf16[96,4608]{1,0:T(8,128)(2,1)S(1)} collective-permute-done((bf16[96,4608]{1,0:T(8,128)(2,1)S(1)}, bf16[96,4608]{1,0:T(8,128)(2,1)S(1)}, u32[]{:S(2)}, u32[]{:S(2)}) %collective-permute-start.42) | collective-permute-done | bytes 884768 | tf_op jit(solution)/shard_map/ppermute | solution.py:95
  229.1 3.2 %collective-permute-start.48 = (bf16[96,1664]{1,0:T(8,128)(2,1)S(1)}, bf16[96,1664]{1,0:T(8,128)(2,1)S(1)}, u32[]{:S(2)}, u32[]{:S(2)}) collective-permute-start(bf16[96,1664]{1,0:T(8,128)(2,1)S(1)} %get-tuple-element.329), channel_id=1, source_target_pairs={{0,16},{1,17},{2,18},{3,19},{4,12},{5,13},{6,14},{7,15},{8,24},{9,... | collective-permute-start | bytes 958472 | tf_op jit(solution)/shard_map/ppermute | solution.py:95
  233.6 3.1 %collective-permute-start.51 = (bf16[24,4608]{1,0:T(8,128)(2,1)S(1)}, bf16[24,4608]{1,0:T(8,128)(2,1)S(1)}, u32[]{:S(2)}, u32[]{:S(2)}) collective-permute-start(bf16[24,4608]{1,0:T(8,128)(2,1)S(1)} %get-tuple-element.335), channel_id=1, source_target_pairs={{0,3},{1,2},{2,1},{3,0},{4,7},{5,6},{6,5},{7,4},{8,11},{9,10},{10,... | collective-permute-start | bytes 663560 | tf_op jit(solution)/shard_map/ppermute | solution.py:100
  239.5 5.5 %collective-permute-done.49.refs_1_ = bf16[24,4608]{1,0:T(8,128)(2,1)S(1)} collective-permute-done((bf16[24,4608]{1,0:T(8,128)(2,1)S(1)}, bf16[24,4608]{1,0:T(8,128)(2,1)S(1)}, u32[]{:S(2)}, u32[]{:S(2)}) %collective-permute-start.49) | collective-permute-done | bytes 221216 | tf_op jit(solution)/shard_map/ppermute | solution.py:100
  245.1 8.7 %collective-permute-done.50.refs_2_ = bf16[24,4608]{1,0:T(8,128)(2,1)S(1)} collective-permute-done((bf16[24,4608]{1,0:T(8,128)(2,1)S(1)}, bf16[24,4608]{1,0:T(8,128)(2,1)S(1)}, u32[]{:S(2)}, u32[]{:S(2)}) %collective-permute-start.50) | collective-permute-done | bytes 221216 | tf_op jit(solution)/shard_map/ppermute | solution.py:100
  (230 shorter events, 92.2 us)
Async XLA Ops:
  8.6 12.2 %collective-permute-start.1 = (bf16[24,2944]{1,0:T(8,128)(2,1)}, bf16[24,2944]{1,0:T(8,128)(2,1)S(1)}, u32[]{:S(2)}, u32[]{:S(2)}) collective-permute-start(bf16[24,2944]{1,0:T(8,128)(2,1)} %pack_first.1.refs_0_), channel_id=1, source_target_pairs={{0,2},{1,3},{2,0},{3,1},{4,6},{5,7},{6,4},{7,5},{8,10},{9,11},{10,... | collective-permute-start | bytes 423944 | tf_op jit(solution)/shard_map/ppermute | solution.py:100
  8.6 12.2 %collective-permute-start = (bf16[24,2944]{1,0:T(8,128)(2,1)}, bf16[24,2944]{1,0:T(8,128)(2,1)S(1)}, u32[]{:S(2)}, u32[]{:S(2)}) collective-permute-start(bf16[24,2944]{1,0:T(8,128)(2,1)} %pack_first.1.refs_0_), channel_id=1, source_target_pairs={{0,1},{1,0},{2,3},{3,2},{4,5},{5,4},{6,7},{7,6},{8,9},{9,8},{10,11... | collective-permute-start | bytes 423944 | tf_op jit(solution)/shard_map/ppermute | solution.py:100
  26.0 13.7 %collective-permute-start.6 = (bf16[24,3328]{1,0:T(8,128)(2,1)}, bf16[24,3328]{1,0:T(8,128)(2,1)S(1)}, u32[]{:S(2)}, u32[]{:S(2)}) collective-permute-start(bf16[24,3328]{1,0:T(8,128)(2,1)} %get-tuple-element.199.refs_0_), channel_id=1, source_target_pairs={{0,2},{1,3},{2,0},{3,1},{4,6},{5,7},{6,4},{7,5},{8,10},{9,11},{10,... | collective-permute-start | bytes 479240 | tf_op jit(solution)/shard_map/ppermute | solution.py:100
  26.0 13.7 %collective-permute-start.5 = (bf16[24,3328]{1,0:T(8,128)(2,1)}, bf16[24,3328]{1,0:T(8,128)(2,1)S(1)}, u32[]{:S(2)}, u32[]{:S(2)}) collective-permute-start(bf16[24,3328]{1,0:T(8,128)(2,1)} %get-tuple-element.199.refs_0_), channel_id=1, source_target_pairs={{0,1},{1,0},{2,3},{3,2},{4,5},{5,4},{6,7},{7,6},{8,9},{9,8},{10,11... | collective-permute-start | bytes 479240 | tf_op jit(solution)/shard_map/ppermute | solution.py:100
  32.0 15.7 %collective-permute-start.8 = (bf16[192,2944]{1,0:T(8,128)(2,1)S(1)}, bf16[192,2944]{1,0:T(8,128)(2,1)S(1)}, u32[]{:S(2)}, u32[]{:S(2)}) collective-permute-start(bf16[192,2944]{1,0:T(8,128)(2,1)S(1)} %stack.60.refs_0_), channel_id=1, source_target_pairs={{0,8},{1,9},{2,10},{3,11},{4,20},{5,21},{6,22},{7,23},{8,0},{9,1},... | collective-permute-start | bytes 3391496 | tf_op jit(solution)/shard_map/ppermute | solution.py:95
  49.8 11.8 %collective-permute-start.11 = (bf16[48,3072]{1,0:T(8,128)(2,1)S(1)}, bf16[48,3072]{1,0:T(8,128)(2,1)S(1)}, u32[]{:S(2)}, u32[]{:S(2)}) collective-permute-start(bf16[48,3072]{1,0:T(8,128)(2,1)S(1)} %get-tuple-element.208), channel_id=1, source_target_pairs={{0,1},{1,0},{2,3},{3,2},{4,5},{5,4},{6,7},{7,6},{8,9},{9,8},{10,11... | collective-permute-start | bytes 884744 | tf_op jit(solution)/shard_map/ppermute | solution.py:100
  49.8 23.2 %collective-permute-start.12 = (bf16[48,3072]{1,0:T(8,128)(2,1)S(1)}, bf16[48,3072]{1,0:T(8,128)(2,1)S(1)}, u32[]{:S(2)}, u32[]{:S(2)}) collective-permute-start(bf16[48,3072]{1,0:T(8,128)(2,1)S(1)} %get-tuple-element.210), channel_id=1, source_target_pairs={{0,2},{1,3},{2,0},{3,1},{4,6},{5,7},{6,4},{7,5},{8,10},{9,11},{10,... | collective-permute-start | bytes 884744 | tf_op jit(solution)/shard_map/ppermute | solution.py:100
  52.9 20.1 %collective-permute-start.13 = (bf16[48,3072]{1,0:T(8,128)(2,1)S(1)}, bf16[48,3072]{1,0:T(8,128)(2,1)S(1)}, u32[]{:S(2)}, u32[]{:S(2)}) collective-permute-start(bf16[48,3072]{1,0:T(8,128)(2,1)S(1)} %get-tuple-element.212), channel_id=1, source_target_pairs={{0,3},{1,2},{2,1},{3,0},{4,7},{5,6},{6,5},{7,4},{8,11},{9,10},{10,... | collective-permute-start | bytes 884744 | tf_op jit(solution)/shard_map/ppermute | solution.py:100
  54.2 33.4 %collective-permute-start.16 = (bf16[384,2944]{1,0:T(8,128)(2,1)S(1)}, bf16[384,2944]{1,0:T(8,128)(2,1)S(1)}, u32[]{:S(2)}, u32[]{:S(2)}) collective-permute-start(bf16[384,2944]{1,0:T(8,128)(2,1)S(1)} %stack.62.refs_1_.refs_9_.refs_10_.refs_5_), channel_id=1, source_target_pairs={{0,4},{1,5},{2,6},{3,7},{4,0},{5,1},{6,2},{7,3},{8,12},{9,13},{10,... | collective-permute-start | bytes 6782984 | tf_op jit(solution)/shard_map/ppermute | solution.py:91
  59.2 27.3 %collective-permute-start.10 = (bf16[192,3328]{1,0:T(8,128)(2,1)S(1)}, bf16[192,3328]{1,0:T(8,128)(2,1)S(1)}, u32[]{:S(2)}, u32[]{:S(2)}) collective-permute-start(bf16[192,3328]{1,0:T(8,128)(2,1)S(1)} %stack.63.refs_0_), channel_id=1, source_target_pairs={{0,8},{1,9},{2,10},{3,11},{4,20},{5,21},{6,22},{7,23},{8,0},{9,1},... | collective-permute-start | bytes 3833864 | tf_op jit(solution)/shard_map/ppermute | solution.py:95
  73.1 16.9 %collective-permute-start.17 = (bf16[192,3072]{1,0:T(8,128)(2,1)S(1)}, bf16[192,3072]{1,0:T(8,128)(2,1)S(1)}, u32[]{:S(2)}, u32[]{:S(2)}) collective-permute-start(bf16[192,3072]{1,0:T(8,128)(2,1)S(1)} %weave.1.refs_0_), channel_id=1, source_target_pairs={{0,16},{1,17},{2,18},{3,19},{4,12},{5,13},{6,14},{7,15},{8,24},{9,... | collective-permute-start | bytes 3538952 | tf_op jit(solution)/shard_map/ppermute | solution.py:95
  74.2 12.6 %collective-permute-start.15 = (bf16[128,768]{1,0:T(8,128)(2,1)S(1)}, bf16[128,768]{1,0:T(8,128)(2,1)S(1)}, u32[]{:S(2)}, u32[]{:S(2)}) collective-permute-start(bf16[128,768]{1,0:T(8,128)(2,1)S(1)} %get-tuple-element.362), channel_id=1, source_target_pairs={{1,0},{2,1},{3,2},{4,3},{5,4},{6,5},{7,6},{8,7},{9,8},{10,9},{11,1... | collective-permute-start | bytes 589832 | tf_op jit(solution)/shard_map/ppermute | solution.py:1151
  90.1 34.8 %collective-permute-start.22 = (bf16[384,3072]{1,0:T(8,128)(2,1)S(1)}, bf16[384,3072]{1,0:T(8,128)(2,1)S(1)}, u32[]{:S(2)}, u32[]{:S(2)}) collective-permute-start(bf16[384,3072]{1,0:T(8,128)(2,1)S(1)} %stack_both.1.refs_0_), channel_id=1, source_target_pairs={{0,8},{1,9},{2,10},{3,11},{4,20},{5,21},{6,22},{7,23},{8,0},{9,1},... | collective-permute-start | bytes 7077896 | tf_op jit(solution)/shard_map/ppermute | solution.py:95
  139.2 20.1 %collective-permute-start.30 = (bf16[192,3072]{1,0:T(8,128)(2,1)S(1)}, bf16[192,3072]{1,0:T(8,128)(2,1)S(1)}, u32[]{:S(2)}, u32[]{:S(2)}) collective-permute-start(bf16[192,3072]{1,0:T(8,128)(2,1)S(1)} %get-tuple-element.272), channel_id=1, source_target_pairs={{0,8},{1,9},{2,10},{3,11},{4,20},{5,21},{6,22},{7,23},{8,0},{9,1},... | collective-permute-start | bytes 3538952 | tf_op jit(solution)/shard_map/ppermute | solution.py:95
  145.5 28.9 %collective-permute-start.33 = (bf16[192,3072]{1,0:T(8,128)(2,1)S(1)}, bf16[192,3072]{1,0:T(8,128)(2,1)S(1)}, u32[]{:S(2)}, u32[]{:S(2)}) collective-permute-start(bf16[192,3072]{1,0:T(8,128)(2,1)S(1)} %get-tuple-element.282), channel_id=1, source_target_pairs={{0,8},{1,9},{2,10},{3,11},{4,20},{5,21},{6,22},{7,23},{8,0},{9,1},... | collective-permute-start | bytes 3538952 | tf_op jit(solution)/shard_map/ppermute | solution.py:95
  159.8 15.0 %collective-permute-start.32 = (bf16[96,3072]{1,0:T(8,128)(2,1)S(1)}, bf16[96,3072]{1,0:T(8,128)(2,1)S(1)}, u32[]{:S(2)}, u32[]{:S(2)}) collective-permute-start(bf16[96,3072]{1,0:T(8,128)(2,1)S(1)} %get-tuple-element.281), channel_id=1, source_target_pairs={{0,16},{1,17},{2,18},{3,19},{4,12},{5,13},{6,14},{7,15},{8,24},{9,... | collective-permute-start | bytes 1769480 | tf_op jit(solution)/shard_map/ppermute | solution.py:95
  174.9 17.0 %collective-permute-start.35 = (bf16[96,3072]{1,0:T(8,128)(2,1)S(1)}, bf16[96,3072]{1,0:T(8,128)(2,1)S(1)}, u32[]{:S(2)}, u32[]{:S(2)}) collective-permute-start(bf16[96,3072]{1,0:T(8,128)(2,1)S(1)} %get-tuple-element.291), channel_id=1, source_target_pairs={{0,16},{1,17},{2,18},{3,19},{4,12},{5,13},{6,14},{7,15},{8,24},{9,... | collective-permute-start | bytes 1769480 | tf_op jit(solution)/shard_map/ppermute | solution.py:95
  178.3 30.2 %collective-permute-start.34 = (bf16[192,4608]{1,0:T(8,128)(2,1)S(1)}, bf16[192,4608]{1,0:T(8,128)(2,1)S(1)}, u32[]{:S(2)}, u32[]{:S(2)}) collective-permute-start(bf16[192,4608]{1,0:T(8,128)(2,1)S(1)} %get-tuple-element.290), channel_id=1, source_target_pairs={{0,8},{1,9},{2,10},{3,11},{4,20},{5,21},{6,22},{7,23},{8,0},{9,1},... | collective-permute-start | bytes 5308424 | tf_op jit(solution)/shard_map/ppermute | solution.py:95
  179.4 14.0 %collective-permute-start.36 = (bf16[24,3072]{1,0:T(8,128)(2,1)S(1)}, bf16[24,3072]{1,0:T(8,128)(2,1)S(1)}, u32[]{:S(2)}, u32[]{:S(2)}) collective-permute-start(bf16[24,3072]{1,0:T(8,128)(2,1)S(1)} %get-tuple-element.303), channel_id=1, source_target_pairs={{0,1},{1,0},{2,3},{3,2},{4,5},{5,4},{6,7},{7,6},{8,9},{9,8},{10,11... | collective-permute-start | bytes 442376 | tf_op jit(solution)/shard_map/ppermute | solution.py:100
  181.6 13.5 %collective-permute-start.37 = (bf16[24,3072]{1,0:T(8,128)(2,1)S(1)}, bf16[24,3072]{1,0:T(8,128)(2,1)S(1)}, u32[]{:S(2)}, u32[]{:S(2)}) collective-permute-start(bf16[24,3072]{1,0:T(8,128)(2,1)S(1)} %get-tuple-element.304), channel_id=1, source_target_pairs={{0,2},{1,3},{2,0},{3,1},{4,6},{5,7},{6,4},{7,5},{8,10},{9,11},{10,... | collective-permute-start | bytes 442376 | tf_op jit(solution)/shard_map/ppermute | solution.py:100
  182.5 17.9 %collective-permute-start.38 = (bf16[24,3072]{1,0:T(8,128)(2,1)S(1)}, bf16[24,3072]{1,0:T(8,128)(2,1)S(1)}, u32[]{:S(2)}, u32[]{:S(2)}) collective-permute-start(bf16[24,3072]{1,0:T(8,128)(2,1)S(1)} %get-tuple-element.305), channel_id=1, source_target_pairs={{0,3},{1,2},{2,1},{3,0},{4,7},{5,6},{6,5},{7,4},{8,11},{9,10},{10,... | collective-permute-start | bytes 442376 | tf_op jit(solution)/shard_map/ppermute | solution.py:100
  193.4 14.4 %collective-permute-start.40 = (bf16[24,3072]{1,0:T(8,128)(2,1)S(1)}, bf16[24,3072]{1,0:T(8,128)(2,1)S(1)}, u32[]{:S(2)}, u32[]{:S(2)}) collective-permute-start(bf16[24,3072]{1,0:T(8,128)(2,1)S(1)} %get-tuple-element.309), channel_id=1, source_target_pairs={{0,2},{1,3},{2,0},{3,1},{4,6},{5,7},{6,4},{7,5},{8,10},{9,11},{10,... | collective-permute-start | bytes 442376 | tf_op jit(solution)/shard_map/ppermute | solution.py:100
  195.2 12.6 %collective-permute-start.41 = (bf16[24,3072]{1,0:T(8,128)(2,1)S(1)}, bf16[24,3072]{1,0:T(8,128)(2,1)S(1)}, u32[]{:S(2)}, u32[]{:S(2)}) collective-permute-start(bf16[24,3072]{1,0:T(8,128)(2,1)S(1)} %get-tuple-element.310), channel_id=1, source_target_pairs={{0,3},{1,2},{2,1},{3,0},{4,7},{5,6},{6,5},{7,4},{8,11},{9,10},{10,... | collective-permute-start | bytes 442376 | tf_op jit(solution)/shard_map/ppermute | solution.py:100
  209.0 19.5 %collective-permute-start.42 = (bf16[96,4608]{1,0:T(8,128)(2,1)S(1)}, bf16[96,4608]{1,0:T(8,128)(2,1)S(1)}, u32[]{:S(2)}, u32[]{:S(2)}) collective-permute-start(bf16[96,4608]{1,0:T(8,128)(2,1)S(1)} %get-tuple-element.314), channel_id=1, source_target_pairs={{0,16},{1,17},{2,18},{3,19},{4,12},{5,13},{6,14},{7,15},{8,24},{9,... | collective-permute-start | bytes 2654216 | tf_op jit(solution)/shard_map/ppermute | solution.py:95
  210.5 18.3 %collective-permute-start.47 = (bf16[192,1664]{1,0:T(8,128)(2,1)S(1)}, bf16[192,1664]{1,0:T(8,128)(2,1)S(1)}, u32[]{:S(2)}, u32[]{:S(2)}) collective-permute-start(bf16[192,1664]{1,0:T(8,128)(2,1)S(1)} %get-tuple-element.326), channel_id=1, source_target_pairs={{0,8},{1,9},{2,10},{3,11},{4,20},{5,21},{6,22},{7,23},{8,0},{9,1},... | collective-permute-start | bytes 1916936 | tf_op jit(solution)/shard_map/ppermute | solution.py:95
  211.4 12.3 %collective-permute-start.46 = (bf16[96,1536]{1,0:T(8,128)(2,1)S(1)}, bf16[96,1536]{1,0:T(8,128)(2,1)S(1)}, u32[]{:S(2)}, u32[]{:S(2)}) collective-permute-start(bf16[96,1536]{1,0:T(8,128)(2,1)S(1)} %get-tuple-element.306), channel_id=1, source_target_pairs={{0,4},{1,5},{2,6},{3,7},{4,0},{5,1},{6,2},{7,3},{8,12},{9,13},{10,... | collective-permute-start | bytes 884744 | tf_op jit(solution)/shard_map/ppermute | solution.py:91
  232.4 12.7 %collective-permute-start.49 = (bf16[24,4608]{1,0:T(8,128)(2,1)S(1)}, bf16[24,4608]{1,0:T(8,128)(2,1)S(1)}, u32[]{:S(2)}, u32[]{:S(2)}) collective-permute-start(bf16[24,4608]{1,0:T(8,128)(2,1)S(1)} %get-tuple-element.333), channel_id=1, source_target_pairs={{0,1},{1,0},{2,3},{3,2},{4,5},{5,4},{6,7},{7,6},{8,9},{9,8},{10,11... | collective-permute-start | bytes 663560 | tf_op jit(solution)/shard_map/ppermute | solution.py:100
  232.8 20.9 %collective-permute-start.50 = (bf16[24,4608]{1,0:T(8,128)(2,1)S(1)}, bf16[24,4608]{1,0:T(8,128)(2,1)S(1)}, u32[]{:S(2)}, u32[]{:S(2)}) collective-permute-start(bf16[24,4608]{1,0:T(8,128)(2,1)S(1)} %get-tuple-element.334), channel_id=1, source_target_pairs={{0,2},{1,3},{2,0},{3,1},{4,6},{5,7},{6,4},{7,5},{8,10},{9,11},{10,... | collective-permute-start | bytes 663560 | tf_op jit(solution)/shard_map/ppermute | solution.py:100
  233.6 20.1 %collective-permute-start.51 = (bf16[24,4608]{1,0:T(8,128)(2,1)S(1)}, bf16[24,4608]{1,0:T(8,128)(2,1)S(1)}, u32[]{:S(2)}, u32[]{:S(2)}) collective-permute-start(bf16[24,4608]{1,0:T(8,128)(2,1)S(1)} %get-tuple-element.335), channel_id=1, source_target_pairs={{0,3},{1,2},{2,1},{3,0},{4,7},{5,6},{6,5},{7,4},{8,11},{9,10},{10,... | collective-permute-start | bytes 663560 | tf_op jit(solution)/shard_map/ppermute | solution.py:100
  237.5 19.4 %collective-permute-start.52 = (bf16[24,1664]{1,0:T(8,128)(2,1)S(1)}, bf16[24,1664]{1,0:T(8,128)(2,1)S(1)}, u32[]{:S(2)}, u32[]{:S(2)}) collective-permute-start(bf16[24,1664]{1,0:T(8,128)(2,1)S(1)} %get-tuple-element.341), channel_id=1, source_target_pairs={{0,1},{1,0},{2,3},{3,2},{4,5},{5,4},{6,7},{7,6},{8,9},{9,8},{10,11... | collective-permute-start | bytes 239624 | tf_op jit(solution)/shard_map/ppermute | solution.py:100
  238.8 20.8 %collective-permute-start.53 = (bf16[24,1664]{1,0:T(8,128)(2,1)S(1)}, bf16[24,1664]{1,0:T(8,128)(2,1)S(1)}, u32[]{:S(2)}, u32[]{:S(2)}) collective-permute-start(bf16[24,1664]{1,0:T(8,128)(2,1)S(1)} %get-tuple-element.342), channel_id=1, source_target_pairs={{0,2},{1,3},{2,0},{3,1},{4,6},{5,7},{6,4},{7,5},{8,10},{9,11},{10,... | collective-permute-start | bytes 239624 | tf_op jit(solution)/shard_map/ppermute | solution.py:100
  245.1 14.5 %collective-permute-start.54 = (bf16[24,1664]{1,0:T(8,128)(2,1)S(1)}, bf16[24,1664]{1,0:T(8,128)(2,1)S(1)}, u32[]{:S(2)}, u32[]{:S(2)}) collective-permute-start(bf16[24,1664]{1,0:T(8,128)(2,1)S(1)} %get-tuple-element.343), channel_id=1, source_target_pairs={{0,3},{1,2},{2,1},{3,0},{4,7},{5,6},{6,5},{7,4},{8,11},{9,10},{10,... | collective-permute-start | bytes 239624 | tf_op jit(solution)/shard_map/ppermute | solution.py:100
  (68 other events, 695.8 us)

commit v2 on v1

--- a/solution.py
+++ b/solution.py
@@ -31,7 +31,7 @@
     "feed_weight": 20,
     "turn": 5.6,
     "routed": 60,
-    "settle_third": 12,
+    "settle_third": 14,
 }
 
 
@@ -867,7 +867,7 @@
             held[seen, beyond] = held[seen, beyond] + tn(probs.astype(BF16), grad_out)
             return carry
 
-        lax.fori_loop(0, HL // 2, pair, 0)
+        lax.fori_loop(0, HL // 2, pair, 0, unroll=2)
     grad_pairs[...] = held[...].astype(BF16)
 
 

time: 261 us -> 265 us (1.015); the launches traced: 261 us -> 261 us
  no operation moved by 1% of the time
where the time goes in v2:
time: 265 us; the launch traced here: 261 us
  waiting for transfers between devices  95.6 us (36%)
  Pallas kernels  79.4 us (30%)
  starting transfers between devices  74.7 us (28%)
  local copies, waits for them, and re-layouts  8.14 us (3%)
    pallas_call x38, Pallas kernels, run(): pl.pallas_call(kernel, name=name, compiler_params=pltpu.CompilerParams(vm...  74.9 us
    ppermute x27, waiting for transfers between devices, by_z(): return lax.ppermute(array, AXES, self.pairs(lambda p, c, z: (p, c, z ^ k)))  64.3 us
    ppermute x27, starting transfers between devices, by_z(): return lax.ppermute(array, AXES, self.pairs(lambda p, c, z: (p, c, z ^ k)))  38.6 us
    ppermute x14, waiting for transfers between devices, by_bit(): lax.ppermute(array, AXES, self.pairs(lambda p, c, z: (p ^ 1 << (j if c el...  24.7 us
    ppermute x14, starting transfers between devices, by_bit(): lax.ppermute(array, AXES, self.pairs(lambda p, c, z: (p ^ 1 << (j if c el...  19.8 us
    ppermute x1, starting transfers between devices, per_device(): above = lax.ppermute(near_tokens[rows - RADIUS:], AXES, step)  6.61 us
    ppermute x1, starting transfers between devices, per_device(): from_prev = lax.ppermute(outer[RADIUS:], AXES, step)  5.61 us
    unnamed x90, local copies, waits for them, and re-layouts  5.4 us
  transfers between devices with their start and end apart: 55, of which 24 were waited for; matrix products, arithmetic and copies ran while one was open for 1% of the time, Pallas kernels for 29%

profile of v2, /device:TPU:0, one launch (start us, length us, event | category | flops | bytes accessed | tf_op | source)
XLA Modules:
  0.0 261.4 jit_solution(17585202851332284873)
XLA Ops:
  3.6 5.0 %collective-permute-start.2 = (bf16[24,2944]{1,0:T(8,128)(2,1)}, bf16[24,2944]{1,0:T(8,128)(2,1)S(1)}, u32[]{:S(2)}, u32[]{:S(2)}) collective-permute-start(bf16[24,2944]{1,0:T(8,128)(2,1)} %pack_first.1.refs_0_), channel_id=1, source_target_pairs={{0,3},{1,2},{2,1},{3,0},{4,7},{5,6},{6,5},{7,4},{8,11},{9,10},{10,... | collective-permute-start | bytes 423944 | tf_op jit(solution)/shard_map/ppermute | solution.py:100
  13.6 7.2 %collective-permute-done.1.refs_2_ = bf16[24,2944]{1,0:T(8,128)(2,1)S(1)} collective-permute-done((bf16[24,2944]{1,0:T(8,128)(2,1)}, bf16[24,2944]{1,0:T(8,128)(2,1)S(1)}, u32[]{:S(2)}, u32[]{:S(2)}) %collective-permute-start.1) | collective-permute-done | bytes 141344 | tf_op jit(solution)/shard_map/ppermute | solution.py:100
  33.5 6.2 %collective-permute-done.6.refs_2_ = bf16[24,3328]{1,0:T(8,128)(2,1)S(1)} collective-permute-done((bf16[24,3328]{1,0:T(8,128)(2,1)}, bf16[24,3328]{1,0:T(8,128)(2,1)S(1)}, u32[]{:S(2)}, u32[]{:S(2)}) %collective-permute-start.6) | collective-permute-done | bytes 159776 | tf_op jit(solution)/shard_map/ppermute | solution.py:100
  41.0 6.8 %collective-permute-done.8.refs_1_ = bf16[192,2944]{1,0:T(8,128)(2,1)S(1)} collective-permute-done((bf16[192,2944]{1,0:T(8,128)(2,1)S(1)}, bf16[192,2944]{1,0:T(8,128)(2,1)S(1)}, u32[]{:S(2)}, u32[]{:S(2)}) %collective-permute-start.8) | collective-permute-done | bytes 1130528 | tf_op jit(solution)/shard_map/ppermute | solution.py:95
  49.8 3.1 %collective-permute-start.12 = (bf16[48,3072]{1,0:T(8,128)(2,1)S(1)}, bf16[48,3072]{1,0:T(8,128)(2,1)S(1)}, u32[]{:S(2)}, u32[]{:S(2)}) collective-permute-start(bf16[48,3072]{1,0:T(8,128)(2,1)S(1)} %get-tuple-element.210), channel_id=1, source_target_pairs={{0,2},{1,3},{2,0},{3,1},{4,6},{5,7},{6,4},{7,5},{8,10},{9,11},{10,... | collective-permute-start | bytes 884744 | tf_op jit(solution)/shard_map/ppermute | solution.py:100
  54.2 4.8 %collective-permute-done.9.refs_1_ = bf16[96,3328]{1,0:T(8,128)(2,1)S(1)} collective-permute-done((bf16[96,3328]{1,0:T(8,128)(2,1)S(1)}, bf16[96,3328]{1,0:T(8,128)(2,1)S(1)}, u32[]{:S(2)}, u32[]{:S(2)}) %collective-permute-start.9) | collective-permute-done | bytes 639008 | tf_op jit(solution)/shard_map/ppermute | solution.py:95
  61.6 11.4 %collective-permute-done.12.refs_2_ = bf16[48,3072]{1,0:T(8,128)(2,1)S(1)} collective-permute-done((bf16[48,3072]{1,0:T(8,128)(2,1)S(1)}, bf16[48,3072]{1,0:T(8,128)(2,1)S(1)}, u32[]{:S(2)}, u32[]{:S(2)}) %collective-permute-start.12) | collective-permute-done | bytes 294944 | tf_op jit(solution)/shard_map/ppermute | solution.py:100
  75.5 6.6 %collective-permute-start.14 = (bf16[128,768]{1,0:T(8,128)(2,1)S(1)}, bf16[128,768]{1,0:T(8,128)(2,1)S(1)}, u32[]{:S(2)}, u32[]{:S(2)}) collective-permute-start(bf16[128,768]{1,0:T(8,128)(2,1)S(1)} %get-tuple-element.363), channel_id=1, source_target_pairs={{0,1},{1,2},{2,3},{3,4},{4,5},{5,6},{6,7},{7,8},{8,9},{9,10},{10,1... | collective-permute-start | bytes 589832 | tf_op jit(solution)/shard_map/ppermute | solution.py:1150
  82.1 4.4 %collective-permute-done.10.refs_1_ = bf16[192,3328]{1,0:T(8,128)(2,1)S(1)} collective-permute-done((bf16[192,3328]{1,0:T(8,128)(2,1)S(1)}, bf16[192,3328]{1,0:T(8,128)(2,1)S(1)}, u32[]{:S(2)}, u32[]{:S(2)}) %collective-permute-start.10) | collective-permute-done | bytes 1277984 | tf_op jit(solution)/shard_map/ppermute | solution.py:95
  92.2 5.7 %light_forward.1 = (bf16[256,512]{1,0:T(8,128)(2,1)S(1)}, f32[256,128]{1,0:T(8,128)S(1)}) custom-call(s32[7]{0:T(128)S(1)} %copy-done.40, bf16[256,512]{1,0:T(8,128)(2,1)S(1)} %get-tuple-element.219.refs_1_.refs_2_, bf16[512,1024]{1,0:T(8,128)(2,1)S(1)} %get-tuple-element.220.refs_2_.refs_3_), custom_call_target="tpu_custom_call" | custom-call | flops 60000002048 | bytes 10000000000 | tf_op jit(solution)/shard_map/light_forward/pallas_call | solution.py:273
  97.9 2.8 %heavy_rows.1.refs_2_ = bf16[1024,768]{1,0:T(8,128)(2,1)S(1)} custom-call(f32[8,768]{1,0:T(8,128)S(1)} %get-tuple-element.226.refs_0_.refs_6_.refs_10_.refs_9_.refs_2_.refs_5_, bf16[768,768]{1,0:T(8,128)(2,1)S(1)} %get-tuple-element.214.refs_1_.refs_0_.refs_8_.refs_12_.refs_10_.refs_3_.refs_6_, bf16[384,3328]{1,0:T(8,128)(2,1)S(1)} %stack.64.refs_2_.refs_3_.refs_11_, ...), custom_call_target="tpu_custom_call" | custom-call | flops 50000000 | bytes 10000000000 | tf_op jit(solution)/shard_map/heavy_rows/pallas_call | solution.py:273
  100.7 4.4 %heavy_pairs.1 = (bf16[1024,1536]{1,0:T(8,128)(2,1)S(1)}, bf16[32,768]{1,0:T(8,128)(2,1)S(1)}, bf16[32,768]{1,0:T(8,128)(2,1)S(1)}) custom-call(bf16[32,256]{1,0:T(8,128)(2,1)S(1)} %get-tuple-element.227.refs_0_.refs_4_.refs_3_.refs_5_, bf16[512,768]{1,0:T(8,128)(2,1)S(1)} %get-tuple-element.228.refs_1_, bf16[1024,768]{1,0:T(8,128)(2,1)S(1)} %heavy_rows.1.refs_2_, ...), custom_call_target="tpu_custom_call" | custom-call | flops 60000002048 | bytes 10000000000 | tf_op jit(solution)/shard_map/heavy_pairs/pallas_call | solution.py:273
  105.2 3.4 %heavy_forward.1 = (bf16[32,768]{1,0:T(8,128)(2,1)S(1)}, f32[64,128]{1,0:T(8,128)S(1)}) custom-call(s32[32,1]{1,0:T(8,128)S(1)} %get-tuple-element.222.refs_0_, s32[1,1024]{1,0:T(1,128)S(1)} %copy-done.38, bf16[32,768]{1,0:T(8,128)(2,1)S(1)} %get-tuple-element.230.refs_2_.refs_6_, bf16[1024,1536]{1,0:T(8,128)(2,1)S(1)} %get-tuple-element.231.refs_3_.refs_5_), custom_call_target="tpu_custom_call" | custom-call | flops 50000000 | bytes 10000000000 | tf_op jit(solution)/shard_map/heavy_forward/pallas_call | solution.py:273
  116.9 3.1 %collective-permute-done.21.refs_3_ = bf16[32,1536]{1,0:T(8,128)(2,1)S(1)} collective-permute-done((bf16[32,1536]{1,0:T(8,128)(2,1)S(1)}, bf16[32,1536]{1,0:T(8,128)(2,1)S(1)}, u32[]{:S(2)}, u32[]{:S(2)}) %collective-permute-start.21) | collective-permute-done | bytes 98336 | tf_op jit(solution)/shard_map/ppermute | solution.py:100
  120.0 4.7 %collective-permute-done.20.refs_2_ = bf16[32,1536]{1,0:T(8,128)(2,1)S(1)} collective-permute-done((bf16[32,1536]{1,0:T(8,128)(2,1)S(1)}, bf16[32,1536]{1,0:T(8,128)(2,1)S(1)}, u32[]{:S(2)}, u32[]{:S(2)}) %collective-permute-start.20) | collective-permute-done | bytes 98336 | tf_op jit(solution)/shard_map/ppermute | solution.py:100
  126.6 5.9 %expert.1 = (bf16[128,1536]{1,0:T(8,128)(2,1)S(1)}, bf16[128,1536]{1,0:T(8,128)(2,1)S(1)}, bf16[192,3072]{1,0:T(8,128)(2,1)S(1)}, bf16[192,3072]{1,0:T(8,128)(2,1)S(1)}) custom-call(bf16[128,1536]{1,0:T(8,128)(2,1)S(1)} %stack.65.refs_0_, bf16[128,1536]{1,0:T(8,128)(2,1)S(1)} %collective-permute-done.23.refs_1_, ...), custom_call_target="tpu_custom_call" | custom-call | flops 60000002048 | bytes 10000000000 | tf_op jit(solution)/shard_map/expert/pallas_call | solution.py:273
  132.7 4.4 %feed.1 = (f32[256,768]{1,0:T(8,128)S(1)}, f32[256,768]{1,0:T(8,128)S(1)}, bf16[256,1024]{1,0:T(8,128)(2,1)S(1)}, bf16[256,2048]{1,0:T(8,128)(2,1)S(1)}) custom-call(bf16[256,768]{1,0:T(8,128)(2,1)S(1)} %get-tuple-element.250.refs_0_, bf16[256,768]{1,0:T(8,128)(2,1)S(1)} %get-tuple-element.201.refs_7_.refs_1_.refs_11_, ...), custom_call_target="tpu_custom_call" | custom-call | flops 60000002048 | bytes 10000000000 | tf_op jit(solution)/shard_map/feed/pallas_call | solution.py:273
  146.3 4.9 %collective-permute-done.28.refs_2_ = bf16[32,1536]{1,0:T(8,128)(2,1)S(1)} collective-permute-done((bf16[32,1536]{1,0:T(8,128)(2,1)S(1)}, bf16[32,1536]{1,0:T(8,128)(2,1)S(1)}, u32[]{:S(2)}, u32[]{:S(2)}) %collective-permute-start.28) | collective-permute-done | bytes 98336 | tf_op jit(solution)/shard_map/ppermute | solution.py:100
  151.3 2.8 %turn.1 = (bf16[256,768]{1,0:T(8,128)(2,1)}, f32[256,768]{1,0:T(8,128)S(1)}, f32[8,768]{1,0:T(8,128)S(1)}) custom-call(bf16[32,1536]{1,0:T(8,128)(2,1)S(1)} %get-tuple-element.256.refs_0_, bf16[32,1536]{1,0:T(8,128)(2,1)S(1)} %collective-permute-done.27.refs_1_, bf16[32,1536]{1,0:T(8,128)(2,1)S(1)} %collective-permute-done.28.refs_2_, ...), custom_call_target="tpu_custom_call" | custom-call | flops 5600000000 | bytes 10000000000 | tf_op jit(solution)/shard_map/turn/pallas_call | solution.py:273
  154.2 5.1 %heavy_scores.1 = (bf16[32,768]{1,0:T(8,128)(2,1)S(1)}, bf16[32,768]{1,0:T(8,128)(2,1)S(1)}, bf16[1024,1536]{1,0:T(8,128)(2,1)S(1)}, f32[32,128]{1,0:T(8,128)S(1)}) custom-call(s32[32,1]{1,0:T(8,128)S(1)} %copy-done.36, s32[1,1024]{1,0:T(1,128)S(1)} %copy-done.39, f32[256,768]{1,0:T(8,128)S(1)} %get-tuple-element.292.refs_2_.refs_0_.refs_1_.refs_3_, ...), custom_call_target="tpu_custom_call" | custom-call | flops 50000000 | bytes 10000000000 | tf_op jit(solution)/shard_map/heavy_scores/pallas_call | solution.py:273
  161.5 9.5 %heavy_weights.1 = (bf16[384,4608]{1,0:T(8,128)(2,1)S(1)}, bf16[384,4608]{1,0:T(8,128)(2,1)S(1)}, f32[8,768]{1,0:T(8,128)S(1)}) custom-call(f32[256,768]{1,0:T(8,128)S(1)} %get-tuple-element.292.refs_2_.refs_0_.refs_1_.refs_3_, bf16[32,768]{1,0:T(8,128)(2,1)S(1)} %copy-done.23, bf16[1024,768]{1,0:T(8,128)(2,1)S(1)} %copy-done.13, ...), custom_call_target="tpu_custom_call" | custom-call | flops 50000000 | bytes 10000000000 | tf_op jit(solution)/shard_map/heavy_weights/pallas_call | solution.py:273
  171.1 3.3 %collective-permute-done.33.refs_2_.refs_3_ = bf16[192,3072]{1,0:T(8,128)(2,1)S(1)} collective-permute-done((bf16[192,3072]{1,0:T(8,128)(2,1)S(1)}, bf16[192,3072]{1,0:T(8,128)(2,1)S(1)}, u32[]{:S(2)}, u32[]{:S(2)}) %collective-permute-start.33) | collective-permute-done | bytes 1179680 | tf_op jit(solution)/shard_map/ppermute | solution.py:95
  184.0 6.7 %light_scores.1 = (bf16[256,512]{1,0:T(8,128)(2,1)S(1)}, bf16[512,1024]{1,0:T(8,128)(2,1)S(1)}) custom-call(s32[7]{0:T(128)S(1)} %copy-done.41, f32[256,768]{1,0:T(8,128)S(1)} %get-tuple-element.292.refs_2_.refs_0_.refs_1_.refs_3_, bf16[256,512]{1,0:T(8,128)(2,1)S(1)} %copy-done.26, bf16[512,1024]{1,0:T(8,128)(2,1)S(1)} %copy-done.16, ...), custom_call_target="tpu_custom_call" | custom-call | flops 50000000 | bytes 10000000000 | tf_op jit(solution)/shard_map/light_scores/pallas_call | solution.py:273
  197.7 3.4 %light_weights.1 = (bf16[384,1664]{1,0:T(8,128)(2,1)S(1)}, bf16[384,1664]{1,0:T(8,128)(2,1)S(1)}, bf16[256,768]{1,0:T(8,128)(2,1)S(1)}, f32[256,768]{1,0:T(8,128)S(1)}) custom-call(bf16[512,768]{1,0:T(8,128)(2,1)S(1)} %copy-done.7, bf16[512,768]{1,0:T(8,128)(2,1)S(1)} %copy-done.20, bf16[256,512]{1,0:T(8,128)(2,1)S(1)} %get-tuple-element.297.refs_2_, ...), custom_call_target="tpu_custom_call" | custom-call | flops 50000000 | bytes 10000000000 | tf_op jit(solution)/shard_map/light_weights/pallas_call | solution.py:273
  201.3 6.5 %collective-permute-done.40.refs_2_ = bf16[24,3072]{1,0:T(8,128)(2,1)S(1)} collective-permute-done((bf16[24,3072]{1,0:T(8,128)(2,1)S(1)}, bf16[24,3072]{1,0:T(8,128)(2,1)S(1)}, u32[]{:S(2)}, u32[]{:S(2)}) %collective-permute-start.40) | collective-permute-done | bytes 147488 | tf_op jit(solution)/shard_map/ppermute | solution.py:100
  212.8 5.6 %collective-permute-start.43 = (bf16[128,768]{1,0:T(8,128)(2,1)S(1)}, bf16[128,768]{1,0:T(8,128)(2,1)S(1)}, u32[]{:S(2)}, u32[]{:S(2)}) collective-permute-start(bf16[128,768]{1,0:T(8,128)(2,1)S(1)} %get-tuple-element.361), channel_id=1, source_target_pairs={{0,1},{1,2},{2,3},{3,4},{4,5},{5,6},{6,7},{7,8},{8,9},{9,10},{10,1... | collective-permute-start | bytes 589832 | tf_op jit(solution)/shard_map/ppermute | solution.py:1390
  218.4 3.6 %collective-permute-done.44.refs_1_ = bf16[128,768]{1,0:T(8,128)(2,1)S(1)} collective-permute-done((bf16[128,768]{1,0:T(8,128)(2,1)S(1)}, bf16[128,768]{1,0:T(8,128)(2,1)S(1)}, u32[]{:S(2)}, u32[]{:S(2)}) %collective-permute-start.44) | collective-permute-done | bytes 196640 | tf_op jit(solution)/shard_map/ppermute | solution.py:1389
  225.3 3.2 %collective-permute-done.42.refs_4_.refs_5_.refs_6_.refs_7_ = bf16[96,4608]{1,0:T(8,128)(2,1)S(1)} collective-permute-done((bf16[96,4608]{1,0:T(8,128)(2,1)S(1)}, bf16[96,4608]{1,0:T(8,128)(2,1)S(1)}, u32[]{:S(2)}, u32[]{:S(2)}) %collective-permute-start.42) | collective-permute-done | bytes 884768 | tf_op jit(solution)/shard_map/ppermute | solution.py:95
  229.1 3.3 %collective-permute-start.48 = (bf16[96,1664]{1,0:T(8,128)(2,1)S(1)}, bf16[96,1664]{1,0:T(8,128)(2,1)S(1)}, u32[]{:S(2)}, u32[]{:S(2)}) collective-permute-start(bf16[96,1664]{1,0:T(8,128)(2,1)S(1)} %get-tuple-element.329), channel_id=1, source_target_pairs={{0,16},{1,17},{2,18},{3,19},{4,12},{5,13},{6,14},{7,15},{8,24},{9,... | collective-permute-start | bytes 958472 | tf_op jit(solution)/shard_map/ppermute | solution.py:95
  233.6 3.1 %collective-permute-start.51 = (bf16[24,4608]{1,0:T(8,128)(2,1)S(1)}, bf16[24,4608]{1,0:T(8,128)(2,1)S(1)}, u32[]{:S(2)}, u32[]{:S(2)}) collective-permute-start(bf16[24,4608]{1,0:T(8,128)(2,1)S(1)} %get-tuple-element.335), channel_id=1, source_target_pairs={{0,3},{1,2},{2,1},{3,0},{4,7},{5,6},{6,5},{7,4},{8,11},{9,10},{10,... | collective-permute-start | bytes 663560 | tf_op jit(solution)/shard_map/ppermute | solution.py:100
  239.5 5.6 %collective-permute-done.49.refs_1_ = bf16[24,4608]{1,0:T(8,128)(2,1)S(1)} collective-permute-done((bf16[24,4608]{1,0:T(8,128)(2,1)S(1)}, bf16[24,4608]{1,0:T(8,128)(2,1)S(1)}, u32[]{:S(2)}, u32[]{:S(2)}) %collective-permute-start.49) | collective-permute-done | bytes 221216 | tf_op jit(solution)/shard_map/ppermute | solution.py:100
  245.1 8.7 %collective-permute-done.50.refs_2_ = bf16[24,4608]{1,0:T(8,128)(2,1)S(1)} collective-permute-done((bf16[24,4608]{1,0:T(8,128)(2,1)S(1)}, bf16[24,4608]{1,0:T(8,128)(2,1)S(1)}, u32[]{:S(2)}, u32[]{:S(2)}) %collective-permute-start.50) | collective-permute-done | bytes 221216 | tf_op jit(solution)/shard_map/ppermute | solution.py:100
  (230 shorter events, 94.1 us)
Async XLA Ops:
  8.6 12.2 %collective-permute-start.1 = (bf16[24,2944]{1,0:T(8,128)(2,1)}, bf16[24,2944]{1,0:T(8,128)(2,1)S(1)}, u32[]{:S(2)}, u32[]{:S(2)}) collective-permute-start(bf16[24,2944]{1,0:T(8,128)(2,1)} %pack_first.1.refs_0_), channel_id=1, source_target_pairs={{0,2},{1,3},{2,0},{3,1},{4,6},{5,7},{6,4},{7,5},{8,10},{9,11},{10,... | collective-permute-start | bytes 423944 | tf_op jit(solution)/shard_map/ppermute | solution.py:100
  8.6 12.2 %collective-permute-start = (bf16[24,2944]{1,0:T(8,128)(2,1)}, bf16[24,2944]{1,0:T(8,128)(2,1)S(1)}, u32[]{:S(2)}, u32[]{:S(2)}) collective-permute-start(bf16[24,2944]{1,0:T(8,128)(2,1)} %pack_first.1.refs_0_), channel_id=1, source_target_pairs={{0,1},{1,0},{2,3},{3,2},{4,5},{5,4},{6,7},{7,6},{8,9},{9,8},{10,11... | collective-permute-start | bytes 423944 | tf_op jit(solution)/shard_map/ppermute | solution.py:100
  26.0 13.7 %collective-permute-start.6 = (bf16[24,3328]{1,0:T(8,128)(2,1)}, bf16[24,3328]{1,0:T(8,128)(2,1)S(1)}, u32[]{:S(2)}, u32[]{:S(2)}) collective-permute-start(bf16[24,3328]{1,0:T(8,128)(2,1)} %get-tuple-element.199.refs_0_), channel_id=1, source_target_pairs={{0,2},{1,3},{2,0},{3,1},{4,6},{5,7},{6,4},{7,5},{8,10},{9,11},{10,... | collective-permute-start | bytes 479240 | tf_op jit(solution)/shard_map/ppermute | solution.py:100
  26.0 13.7 %collective-permute-start.5 = (bf16[24,3328]{1,0:T(8,128)(2,1)}, bf16[24,3328]{1,0:T(8,128)(2,1)S(1)}, u32[]{:S(2)}, u32[]{:S(2)}) collective-permute-start(bf16[24,3328]{1,0:T(8,128)(2,1)} %get-tuple-element.199.refs_0_), channel_id=1, source_target_pairs={{0,1},{1,0},{2,3},{3,2},{4,5},{5,4},{6,7},{7,6},{8,9},{9,8},{10,11... | collective-permute-start | bytes 479240 | tf_op jit(solution)/shard_map/ppermute | solution.py:100
  32.0 15.7 %collective-permute-start.8 = (bf16[192,2944]{1,0:T(8,128)(2,1)S(1)}, bf16[192,2944]{1,0:T(8,128)(2,1)S(1)}, u32[]{:S(2)}, u32[]{:S(2)}) collective-permute-start(bf16[192,2944]{1,0:T(8,128)(2,1)S(1)} %stack.60.refs_0_), channel_id=1, source_target_pairs={{0,8},{1,9},{2,10},{3,11},{4,20},{5,21},{6,22},{7,23},{8,0},{9,1},... | collective-permute-start | bytes 3391496 | tf_op jit(solution)/shard_map/ppermute | solution.py:95
  49.8 11.8 %collective-permute-start.11 = (bf16[48,3072]{1,0:T(8,128)(2,1)S(1)}, bf16[48,3072]{1,0:T(8,128)(2,1)S(1)}, u32[]{:S(2)}, u32[]{:S(2)}) collective-permute-start(bf16[48,3072]{1,0:T(8,128)(2,1)S(1)} %get-tuple-element.208), channel_id=1, source_target_pairs={{0,1},{1,0},{2,3},{3,2},{4,5},{5,4},{6,7},{7,6},{8,9},{9,8},{10,11... | collective-permute-start | bytes 884744 | tf_op jit(solution)/shard_map/ppermute | solution.py:100
  49.8 23.2 %collective-permute-start.12 = (bf16[48,3072]{1,0:T(8,128)(2,1)S(1)}, bf16[48,3072]{1,0:T(8,128)(2,1)S(1)}, u32[]{:S(2)}, u32[]{:S(2)}) collective-permute-start(bf16[48,3072]{1,0:T(8,128)(2,1)S(1)} %get-tuple-element.210), channel_id=1, source_target_pairs={{0,2},{1,3},{2,0},{3,1},{4,6},{5,7},{6,4},{7,5},{8,10},{9,11},{10,... | collective-permute-start | bytes 884744 | tf_op jit(solution)/shard_map/ppermute | solution.py:100
  52.9 20.1 %collective-permute-start.13 = (bf16[48,3072]{1,0:T(8,128)(2,1)S(1)}, bf16[48,3072]{1,0:T(8,128)(2,1)S(1)}, u32[]{:S(2)}, u32[]{:S(2)}) collective-permute-start(bf16[48,3072]{1,0:T(8,128)(2,1)S(1)} %get-tuple-element.212), channel_id=1, source_target_pairs={{0,3},{1,2},{2,1},{3,0},{4,7},{5,6},{6,5},{7,4},{8,11},{9,10},{10,... | collective-permute-start | bytes 884744 | tf_op jit(solution)/shard_map/ppermute | solution.py:100
  54.2 33.4 %collective-permute-start.16 = (bf16[384,2944]{1,0:T(8,128)(2,1)S(1)}, bf16[384,2944]{1,0:T(8,128)(2,1)S(1)}, u32[]{:S(2)}, u32[]{:S(2)}) collective-permute-start(bf16[384,2944]{1,0:T(8,128)(2,1)S(1)} %stack.62.refs_1_.refs_9_.refs_10_.refs_5_), channel_id=1, source_target_pairs={{0,4},{1,5},{2,6},{3,7},{4,0},{5,1},{6,2},{7,3},{8,12},{9,13},{10,... | collective-permute-start | bytes 6782984 | tf_op jit(solution)/shard_map/ppermute | solution.py:91
  59.2 27.3 %collective-permute-start.10 = (bf16[192,3328]{1,0:T(8,128)(2,1)S(1)}, bf16[192,3328]{1,0:T(8,128)(2,1)S(1)}, u32[]{:S(2)}, u32[]{:S(2)}) collective-permute-start(bf16[192,3328]{1,0:T(8,128)(2,1)S(1)} %stack.63.refs_0_), channel_id=1, source_target_pairs={{0,8},{1,9},{2,10},{3,11},{4,20},{5,21},{6,22},{7,23},{8,0},{9,1},... | collective-permute-start | bytes 3833864 | tf_op jit(solution)/shard_map/ppermute | solution.py:95
  73.1 16.9 %collective-permute-start.17 = (bf16[192,3072]{1,0:T(8,128)(2,1)S(1)}, bf16[192,3072]{1,0:T(8,128)(2,1)S(1)}, u32[]{:S(2)}, u32[]{:S(2)}) collective-permute-start(bf16[192,3072]{1,0:T(8,128)(2,1)S(1)} %weave.1.refs_0_), channel_id=1, source_target_pairs={{0,16},{1,17},{2,18},{3,19},{4,12},{5,13},{6,14},{7,15},{8,24},{9,... | collective-permute-start | bytes 3538952 | tf_op jit(solution)/shard_map/ppermute | solution.py:95
  74.2 12.6 %collective-permute-start.15 = (bf16[128,768]{1,0:T(8,128)(2,1)S(1)}, bf16[128,768]{1,0:T(8,128)(2,1)S(1)}, u32[]{:S(2)}, u32[]{:S(2)}) collective-permute-start(bf16[128,768]{1,0:T(8,128)(2,1)S(1)} %get-tuple-element.362), channel_id=1, source_target_pairs={{1,0},{2,1},{3,2},{4,3},{5,4},{6,5},{7,6},{8,7},{9,8},{10,9},{11,1... | collective-permute-start | bytes 589832 | tf_op jit(solution)/shard_map/ppermute | solution.py:1151
  90.1 34.8 %collective-permute-start.22 = (bf16[384,3072]{1,0:T(8,128)(2,1)S(1)}, bf16[384,3072]{1,0:T(8,128)(2,1)S(1)}, u32[]{:S(2)}, u32[]{:S(2)}) collective-permute-start(bf16[384,3072]{1,0:T(8,128)(2,1)S(1)} %stack_both.1.refs_0_), channel_id=1, source_target_pairs={{0,8},{1,9},{2,10},{3,11},{4,20},{5,21},{6,22},{7,23},{8,0},{9,1},... | collective-permute-start | bytes 7077896 | tf_op jit(solution)/shard_map/ppermute | solution.py:95
  139.2 20.1 %collective-permute-start.30 = (bf16[192,3072]{1,0:T(8,128)(2,1)S(1)}, bf16[192,3072]{1,0:T(8,128)(2,1)S(1)}, u32[]{:S(2)}, u32[]{:S(2)}) collective-permute-start(bf16[192,3072]{1,0:T(8,128)(2,1)S(1)} %get-tuple-element.272), channel_id=1, source_target_pairs={{0,8},{1,9},{2,10},{3,11},{4,20},{5,21},{6,22},{7,23},{8,0},{9,1},... | collective-permute-start | bytes 3538952 | tf_op jit(solution)/shard_map/ppermute | solution.py:95
  145.5 28.9 %collective-permute-start.33 = (bf16[192,3072]{1,0:T(8,128)(2,1)S(1)}, bf16[192,3072]{1,0:T(8,128)(2,1)S(1)}, u32[]{:S(2)}, u32[]{:S(2)}) collective-permute-start(bf16[192,3072]{1,0:T(8,128)(2,1)S(1)} %get-tuple-element.282), channel_id=1, source_target_pairs={{0,8},{1,9},{2,10},{3,11},{4,20},{5,21},{6,22},{7,23},{8,0},{9,1},... | collective-permute-start | bytes 3538952 | tf_op jit(solution)/shard_map/ppermute | solution.py:95
  159.8 15.0 %collective-permute-start.32 = (bf16[96,3072]{1,0:T(8,128)(2,1)S(1)}, bf16[96,3072]{1,0:T(8,128)(2,1)S(1)}, u32[]{:S(2)}, u32[]{:S(2)}) collective-permute-start(bf16[96,3072]{1,0:T(8,128)(2,1)S(1)} %get-tuple-element.281), channel_id=1, source_target_pairs={{0,16},{1,17},{2,18},{3,19},{4,12},{5,13},{6,14},{7,15},{8,24},{9,... | collective-permute-start | bytes 1769480 | tf_op jit(solution)/shard_map/ppermute | solution.py:95
  174.9 15.8 %collective-permute-start.35 = (bf16[96,3072]{1,0:T(8,128)(2,1)S(1)}, bf16[96,3072]{1,0:T(8,128)(2,1)S(1)}, u32[]{:S(2)}, u32[]{:S(2)}) collective-permute-start(bf16[96,3072]{1,0:T(8,128)(2,1)S(1)} %get-tuple-element.291), channel_id=1, source_target_pairs={{0,16},{1,17},{2,18},{3,19},{4,12},{5,13},{6,14},{7,15},{8,24},{9,... | collective-permute-start | bytes 1769480 | tf_op jit(solution)/shard_map/ppermute | solution.py:95
  178.3 30.2 %collective-permute-start.34 = (bf16[192,4608]{1,0:T(8,128)(2,1)S(1)}, bf16[192,4608]{1,0:T(8,128)(2,1)S(1)}, u32[]{:S(2)}, u32[]{:S(2)}) collective-permute-start(bf16[192,4608]{1,0:T(8,128)(2,1)S(1)} %get-tuple-element.290), channel_id=1, source_target_pairs={{0,8},{1,9},{2,10},{3,11},{4,20},{5,21},{6,22},{7,23},{8,0},{9,1},... | collective-permute-start | bytes 5308424 | tf_op jit(solution)/shard_map/ppermute | solution.py:95
  179.4 12.8 %collective-permute-start.36 = (bf16[24,3072]{1,0:T(8,128)(2,1)S(1)}, bf16[24,3072]{1,0:T(8,128)(2,1)S(1)}, u32[]{:S(2)}, u32[]{:S(2)}) collective-permute-start(bf16[24,3072]{1,0:T(8,128)(2,1)S(1)} %get-tuple-element.303), channel_id=1, source_target_pairs={{0,1},{1,0},{2,3},{3,2},{4,5},{5,4},{6,7},{7,6},{8,9},{9,8},{10,11... | collective-permute-start | bytes 442376 | tf_op jit(solution)/shard_map/ppermute | solution.py:100
  181.6 14.7 %collective-permute-start.37 = (bf16[24,3072]{1,0:T(8,128)(2,1)S(1)}, bf16[24,3072]{1,0:T(8,128)(2,1)S(1)}, u32[]{:S(2)}, u32[]{:S(2)}) collective-permute-start(bf16[24,3072]{1,0:T(8,128)(2,1)S(1)} %get-tuple-element.304), channel_id=1, source_target_pairs={{0,2},{1,3},{2,0},{3,1},{4,6},{5,7},{6,4},{7,5},{8,10},{9,11},{10,... | collective-permute-start | bytes 442376 | tf_op jit(solution)/shard_map/ppermute | solution.py:100
  182.5 18.7 %collective-permute-start.38 = (bf16[24,3072]{1,0:T(8,128)(2,1)S(1)}, bf16[24,3072]{1,0:T(8,128)(2,1)S(1)}, u32[]{:S(2)}, u32[]{:S(2)}) collective-permute-start(bf16[24,3072]{1,0:T(8,128)(2,1)S(1)} %get-tuple-element.305), channel_id=1, source_target_pairs={{0,3},{1,2},{2,1},{3,0},{4,7},{5,6},{6,5},{7,4},{8,11},{9,10},{10,... | collective-permute-start | bytes 442376 | tf_op jit(solution)/shard_map/ppermute | solution.py:100
  192.1 15.6 %collective-permute-start.40 = (bf16[24,3072]{1,0:T(8,128)(2,1)S(1)}, bf16[24,3072]{1,0:T(8,128)(2,1)S(1)}, u32[]{:S(2)}, u32[]{:S(2)}) collective-permute-start(bf16[24,3072]{1,0:T(8,128)(2,1)S(1)} %get-tuple-element.309), channel_id=1, source_target_pairs={{0,2},{1,3},{2,0},{3,1},{4,6},{5,7},{6,4},{7,5},{8,10},{9,11},{10,... | collective-permute-start | bytes 442376 | tf_op jit(solution)/shard_map/ppermute | solution.py:100
  196.3 11.4 %collective-permute-start.41 = (bf16[24,3072]{1,0:T(8,128)(2,1)S(1)}, bf16[24,3072]{1,0:T(8,128)(2,1)S(1)}, u32[]{:S(2)}, u32[]{:S(2)}) collective-permute-start(bf16[24,3072]{1,0:T(8,128)(2,1)S(1)} %get-tuple-element.310), channel_id=1, source_target_pairs={{0,3},{1,2},{2,1},{3,0},{4,7},{5,6},{6,5},{7,4},{8,11},{9,10},{10,... | collective-permute-start | bytes 442376 | tf_op jit(solution)/shard_map/ppermute | solution.py:100
  209.0 19.5 %collective-permute-start.42 = (bf16[96,4608]{1,0:T(8,128)(2,1)S(1)}, bf16[96,4608]{1,0:T(8,128)(2,1)S(1)}, u32[]{:S(2)}, u32[]{:S(2)}) collective-permute-start(bf16[96,4608]{1,0:T(8,128)(2,1)S(1)} %get-tuple-element.314), channel_id=1, source_target_pairs={{0,16},{1,17},{2,18},{3,19},{4,12},{5,13},{6,14},{7,15},{8,24},{9,... | collective-permute-start | bytes 2654216 | tf_op jit(solution)/shard_map/ppermute | solution.py:95
  210.5 18.2 %collective-permute-start.47 = (bf16[192,1664]{1,0:T(8,128)(2,1)S(1)}, bf16[192,1664]{1,0:T(8,128)(2,1)S(1)}, u32[]{:S(2)}, u32[]{:S(2)}) collective-permute-start(bf16[192,1664]{1,0:T(8,128)(2,1)S(1)} %get-tuple-element.326), channel_id=1, source_target_pairs={{0,8},{1,9},{2,10},{3,11},{4,20},{5,21},{6,22},{7,23},{8,0},{9,1},... | collective-permute-start | bytes 1916936 | tf_op jit(solution)/shard_map/ppermute | solution.py:95
  211.4 12.3 %collective-permute-start.46 = (bf16[96,1536]{1,0:T(8,128)(2,1)S(1)}, bf16[96,1536]{1,0:T(8,128)(2,1)S(1)}, u32[]{:S(2)}, u32[]{:S(2)}) collective-permute-start(bf16[96,1536]{1,0:T(8,128)(2,1)S(1)} %get-tuple-element.306), channel_id=1, source_target_pairs={{0,4},{1,5},{2,6},{3,7},{4,0},{5,1},{6,2},{7,3},{8,12},{9,13},{10,... | collective-permute-start | bytes 884744 | tf_op jit(solution)/shard_map/ppermute | solution.py:91
  232.4 12.7 %collective-permute-start.49 = (bf16[24,4608]{1,0:T(8,128)(2,1)S(1)}, bf16[24,4608]{1,0:T(8,128)(2,1)S(1)}, u32[]{:S(2)}, u32[]{:S(2)}) collective-permute-start(bf16[24,4608]{1,0:T(8,128)(2,1)S(1)} %get-tuple-element.333), channel_id=1, source_target_pairs={{0,1},{1,0},{2,3},{3,2},{4,5},{5,4},{6,7},{7,6},{8,9},{9,8},{10,11... | collective-permute-start | bytes 663560 | tf_op jit(solution)/shard_map/ppermute | solution.py:100
  232.8 20.9 %collective-permute-start.50 = (bf16[24,4608]{1,0:T(8,128)(2,1)S(1)}, bf16[24,4608]{1,0:T(8,128)(2,1)S(1)}, u32[]{:S(2)}, u32[]{:S(2)}) collective-permute-start(bf16[24,4608]{1,0:T(8,128)(2,1)S(1)} %get-tuple-element.334), channel_id=1, source_target_pairs={{0,2},{1,3},{2,0},{3,1},{4,6},{5,7},{6,4},{7,5},{8,10},{9,11},{10,... | collective-permute-start | bytes 663560 | tf_op jit(solution)/shard_map/ppermute | solution.py:100
  233.6 20.1 %collective-permute-start.51 = (bf16[24,4608]{1,0:T(8,128)(2,1)S(1)}, bf16[24,4608]{1,0:T(8,128)(2,1)S(1)}, u32[]{:S(2)}, u32[]{:S(2)}) collective-permute-start(bf16[24,4608]{1,0:T(8,128)(2,1)S(1)} %get-tuple-element.335), channel_id=1, source_target_pairs={{0,3},{1,2},{2,1},{3,0},{4,7},{5,6},{6,5},{7,4},{8,11},{9,10},{10,... | collective-permute-start | bytes 663560 | tf_op jit(solution)/shard_map/ppermute | solution.py:100
  237.5 19.4 %collective-permute-start.52 = (bf16[24,1664]{1,0:T(8,128)(2,1)S(1)}, bf16[24,1664]{1,0:T(8,128)(2,1)S(1)}, u32[]{:S(2)}, u32[]{:S(2)}) collective-permute-start(bf16[24,1664]{1,0:T(8,128)(2,1)S(1)} %get-tuple-element.341), channel_id=1, source_target_pairs={{0,1},{1,0},{2,3},{3,2},{4,5},{5,4},{6,7},{7,6},{8,9},{9,8},{10,11... | collective-permute-start | bytes 239624 | tf_op jit(solution)/shard_map/ppermute | solution.py:100
  238.7 20.8 %collective-permute-start.53 = (bf16[24,1664]{1,0:T(8,128)(2,1)S(1)}, bf16[24,1664]{1,0:T(8,128)(2,1)S(1)}, u32[]{:S(2)}, u32[]{:S(2)}) collective-permute-start(bf16[24,1664]{1,0:T(8,128)(2,1)S(1)} %get-tuple-element.342), channel_id=1, source_target_pairs={{0,2},{1,3},{2,0},{3,1},{4,6},{5,7},{6,4},{7,5},{8,10},{9,11},{10,... | collective-permute-start | bytes 239624 | tf_op jit(solution)/shard_map/ppermute | solution.py:100
  245.1 14.5 %collective-permute-start.54 = (bf16[24,1664]{1,0:T(8,128)(2,1)S(1)}, bf16[24,1664]{1,0:T(8,128)(2,1)S(1)}, u32[]{:S(2)}, u32[]{:S(2)}) collective-permute-start(bf16[24,1664]{1,0:T(8,128)(2,1)S(1)} %get-tuple-element.343), channel_id=1, source_target_pairs={{0,3},{1,2},{2,1},{3,0},{4,7},{5,6},{6,5},{7,4},{8,11},{9,10},{10,... | collective-permute-start | bytes 239624 | tf_op jit(solution)/shard_map/ppermute | solution.py:100
  (68 other events, 700.9 us)
